TPU v7x, 128 devices: a whole 4x4x4 slice. The times are simulated.
128 devices in a mesh: wide: 8 (over y, core), narrow: 16 (over x, z).
Axes of the slice: x: 4, y: 4, z: 4, core: 2. Of those that a mesh axis runs over, the one named last changes fastest.
Arguments:
- samples: bfloat16 [16384, 1024], P(('wide', 'narrow')), may hold values from -6 to 6
- clusters: int32 [16384, 4], P(('wide', 'narrow')), may hold values from 0 to 16383, all different within a row
- blocks: int32 [16384, 8], P(('wide', 'narrow')), may hold values from 0 to 127, all different within a row; in each aligned block of 128 rows (0 to 127, 128 to 255, ...) at most 10 rows name the same one
- labels: int32 [16384, 8], P(('wide', 'narrow')), may hold values from 0 to 2047
- coarse_weight: bfloat16 [1024, 16384], P(None, 'narrow'), may hold values from -0.1875 to 0.1875
- coarse_moment: float32 [1024, 16384], P('wide', 'narrow'), may hold values from -180 to 180
- fine_weight: bfloat16 [128, 1024, 2048], P(('wide', 'narrow')), may hold values from -0.1875 to 0.1875
- fine_moment: float32 [128, 1024, 2048], P(('wide', 'narrow')), may hold values from -60 to 60
Outputs:
- row_grads: float32 [16384, 1024], P(('wide', 'narrow'))
- new_coarse: float32 [1024, 16384], P('wide', 'narrow')
- new_fine: float32 [128, 1024, 2048], P(('wide', 'narrow'))
Inputs may be any that keep to these rules, and one draw needn't show every extreme that they name: Each row names 4 different clusters. Each row names 8 different fine blocks; among the rows of one device no block is named more than 10 times, and some block is named exactly 10 times.
All inputs are finite; a program needn't handle non-finite values.
Results may differ from a plain program's by a relative error of at most 0.0023.
Values may be sent and summed in bfloat16 or wider, within the bound.
No kernel may reach another device: no remote copies, remote signals or barrier semaphores. Data moves between devices by JAX's collectives and lax.ppermute only.
A program may use at most 192 MiB of HBM per device.

v0:
```python
import functools

import jax
import jax.numpy as jnp
from jax import lax
from jax.experimental import pallas as pl
from jax.experimental.pallas import tpu as pltpu
from jax.sharding import PartitionSpec as P


BETA = 0.9
AXES = ("wide", "narrow")
SIDE = 4
STEPS = (0, 1, -1, 2)
DIGIT = 128
F32, BF16 = jnp.float32, jnp.bfloat16


def device_map(move):
    pairs = []
    for y in range(SIDE):
        for core in range(2):
            for x in range(SIDE):
                for z in range(SIDE):
                    tx, ty, tz, tc = move(x, y, z, core)
                    target = ((ty % SIDE) * 2 + tc) * 16 + (tx % SIDE) * 4 + tz % SIDE
                    pairs.append(((y * 2 + core) * 16 + x * 4 + z, target))
    return pairs


def first_line(step):
    return device_map(lambda x, y, z, c: (x, y, z + step, c) if c == 0 else (x + step, y, z, c))


def second_line(step):
    return device_map(lambda x, y, z, c: (x + step, y, z, c) if c == 0 else (x, y, z + step, c))


def column_map(step):
    return device_map(lambda x, y, z, c: (x, y + step, z, c))


def partner_map():
    return device_map(lambda x, y, z, c: (x, y, z, 1 - c))


def send(value, pairs):
    return lax.ppermute(value, AXES, pairs)


def after(value, *earlier):
    return lax.optimization_barrier((value, *earlier))[0]


def swap_wide(value):
    return lax.all_to_all(value, "wide", split_axis=0, concat_axis=0, tiled=True)


def sigmoid(x):
    return 0.5 * jnp.tanh(0.5 * x) + 0.5


def dot(a, b, left, right):
    return lax.dot_general(a, b, (((left,), (right,)), ((), ())), preferred_element_type=F32)


def stored(shape):
    if isinstance(shape, tuple):
        return tuple(stored(one) for one in shape)
    return pltpu.HBM(shape.shape, shape.dtype)


def call(body, grid, in_specs, out_specs, out_shape, flops, scratch=(), aliases=None):
    return pl.pallas_call(
        body,
        grid=grid,
        in_specs=in_specs,
        out_specs=out_specs,
        out_shape=stored(out_shape),
        scratch_shapes=scratch,
        input_output_aliases=aliases or {},
        compiler_params=pltpu.CompilerParams(vmem_limit_bytes=48 << 20),
        cost_estimate=pl.CostEstimate(flops=flops, transcendentals=0, bytes_accessed=flops // 1000),
    )


def whole(array):
    return pl.BlockSpec(array.shape, lambda i: (0,) * array.ndim)


def selection(slots, size):
    count, rows = slots.shape
    table = jnp.concatenate(
        [jnp.broadcast_to(slots[q : q + 1], (size, rows)) for q in range(count)], axis=0
    )
    place = lax.broadcasted_iota(jnp.int32, (size, 1), 0)
    place = jnp.concatenate([place] * count, axis=0)
    return (table == place).astype(F32).astype(BF16)


def compact_body(row_ref, slot_ref, *refs):
    out_ref = refs[-1]
    count, size = out_ref.shape[:2]
    picked = dot(selection(slot_ref[...], size), row_ref[...], 1, 0)
    for q in range(count):
        out_ref[q] = picked[q * size : (q + 1) * size].astype(BF16)


def compact(rows, slots, message, place, size, total):
    count, width = slots.shape[0], rows.shape[1]
    earlier = () if message is None else (message,)
    return call(
        compact_body,
        (1,),
        [whole(rows), whole(slots)] + [pl.BlockSpec(memory_space=pl.ANY) for _ in earlier],
        pl.BlockSpec((count, size, width), lambda i: (0, place, 0)),
        jax.ShapeDtypeStruct((count, total, width), BF16),
        2 * count * size * width * rows.shape[0],
        aliases={2: 0} if earlier else None,
    )(rows, slots, *earlier)


def prepare_body(picked, capacity, mine_ref, *refs):
    notes, (slot_ref, spare_ref) = refs[:-2], refs[-2:]
    sources, _, rows = notes[0].shape
    count = mine_ref.shape[0]
    mine = mine_ref[...]
    hits, tags = [], []
    for note in notes:
        for j in range(sources):
            hit = jnp.zeros((count, rows), F32)
            tag = jnp.zeros((count, rows), F32)
            for k in range(picked):
                same = note[j, k : k + 1, :] == mine
                label = note[j, picked + k : picked + k + 1, :].astype(F32) + 1.0
                hit = jnp.where(same, 1.0, hit)
                tag = jnp.where(same, jnp.broadcast_to(label, tag.shape), tag)
            hits.append(hit)
            tags.append(tag)
    one = lax.broadcasted_iota(jnp.int32, (rows, rows), 0)
    two = lax.broadcasted_iota(jnp.int32, (rows, rows), 1)
    before = (one < two).astype(F32).astype(BF16)
    places = dot(jnp.concatenate(hits, axis=0).astype(BF16), before, 1, 0)
    spare_ref[...] = jnp.zeros(spare_ref.shape, spare_ref.dtype)
    size = sources * capacity
    for k in range(len(notes)):
        for j in range(sources):
            at = k * sources + j
            place = places[at * count : (at + 1) * count] + float(j * capacity)
            slot = jnp.where(hits[at] > 0.0, place, -1.0)
            slot_ref[k, :, j * rows : (j + 1) * rows] = slot.astype(jnp.int32)
        tag = jnp.concatenate(tags[k * sources : (k + 1) * sources], axis=1)
        high = jnp.floor(tag * (1.0 / DIGIT))
        digits = jnp.concatenate([high, tag - high * DIGIT], axis=0).astype(BF16)
        found = dot(digits, selection(slot_ref[k], size), 1, 1)
        owner = lax.broadcasted_iota(jnp.int32, found.shape, 0)
        owner = jnp.where(owner >= count, owner - count, owner)
        lane = lax.broadcasted_iota(jnp.int32, found.shape, 1) - owner * size
        found = jnp.where((lane >= 0) & (lane < size), found, 0.0)
        spare_ref[k : k + 1, : count * size] = jnp.sum(found[:count], axis=0, keepdims=True)
        low = jnp.sum(found[count:], axis=0, keepdims=True)
        spare_ref[len(notes) + k : len(notes) + k + 1, : count * size] = low


def prepare(mine, notes, picked, capacity, width):
    sources, _, rows = notes[0].shape
    out = (
        jax.ShapeDtypeStruct((len(notes), mine.shape[0], sources * rows), jnp.int32),
        jax.ShapeDtypeStruct((2 * len(notes), width), F32),
    )
    inputs = [mine, *notes]
    return call(
        functools.partial(prepare_body, picked, capacity),
        (1,),
        [whole(a) for a in inputs],
        tuple(whole(a) for a in out),
        out,
        1 << 28,
    )(*inputs)


def stamp_body(spare_ref, out_ref):
    for q in range(out_ref.shape[0]):
        out_ref[q] = spare_ref[...].astype(BF16)


def stamp(spare, count, size):
    lines, width = spare.shape
    last = size // lines
    return call(
        stamp_body,
        (1,),
        [whole(spare)],
        pl.BlockSpec((count, lines, width), lambda i: (0, last, 0)),
        jax.ShapeDtypeStruct((count, size + lines, width), BF16),
        1 << 20,
    )(spare)


def coarse_body(
    steps, top, row_ref, weight_ref, note_ref, id_ref, grad_ref, part_ref, total_ref, name_ref
):
    step = pl.program_id(0)
    rows = note_ref.shape[2]

    @pl.when(step == 0)
    def _():
        for j in range(note_ref.shape[0]):
            name_ref[j * rows : (j + 1) * rows, :] = note_ref[j, -8:, :].astype(F32).T

    weight = weight_ref[...]
    logits = dot(row_ref[...], weight, 1, 0)
    names, ids = name_ref[...], id_ref[...]
    target = names[:, 0:1] == ids
    for t in range(1, top):
        target = target | (names[:, t : t + 1] == ids)
    grad = sigmoid(logits)
    grad = jnp.where(target, grad - 1.0, grad).astype(BF16)
    grad_ref[...] = grad
    part = dot(grad, weight, 1, 1)

    @pl.when(step == 0)
    def _():
        total_ref[...] = part

    @pl.when((step > 0) & (step < steps - 1))
    def _():
        total_ref[...] += part

    @pl.when(step == steps - 1)
    def _():
        part_ref[...] = (total_ref[...] + part).astype(part_ref.dtype)


def coarse(rows, weight, notes, ids, top, dtype, tile=512):
    count, width = rows.shape
    columns = weight.shape[1]
    steps = columns // tile
    return call(
        functools.partial(coarse_body, steps, top),
        (steps,),
        [
            whole(rows),
            pl.BlockSpec((width, tile), lambda i: (0, i)),
            whole(notes),
            pl.BlockSpec((1, tile), lambda i: (0, i)),
        ],
        (
            pl.BlockSpec((count, tile), lambda i: (0, i)),
            pl.BlockSpec((count, width), lambda i: (0, 0)),
        ),
        (
            jax.ShapeDtypeStruct((count, columns), BF16),
            jax.ShapeDtypeStruct((count, width), dtype),
        ),
        4 * count * width * columns,
        [pltpu.VMEM((count, width), F32), pltpu.VMEM((count, 8), F32)],
    )(rows, weight, notes, ids)


def fine_step(row_ref, weight_ref, grad_ref, total_ref, here_ref):
    step = pl.program_id(0)
    weight = weight_ref[0]
    logits = dot(row_ref[...], weight, 1, 0)
    label = here_ref[...].astype(jnp.int32)
    ids = lax.broadcasted_iota(jnp.int32, logits.shape, 1) + step * logits.shape[1]
    grad = sigmoid(logits)
    grad = jnp.where(label == ids, grad - 1.0, grad)
    grad = jnp.where(label >= 0, grad, 0.0).astype(BF16)
    grad_ref[...] = grad
    part = dot(grad, weight, 1, 1)

    @pl.when(step == 0)
    def _():
        total_ref[...] = part

    @pl.when(step > 0)
    def _():
        total_ref[...] += part


def fine_first_body(
    steps, count, group, row_ref, weight_ref, seat_ref, grad_ref, pair_ref, next_ref, total_ref, here_ref
):
    size = row_ref.shape[0] // count
    rest = next_ref.shape[0] // count

    @pl.when(pl.program_id(0) == 0)
    def _():
        span = count * group
        lane = lax.broadcasted_iota(jnp.int32, (group, span), 1)
        lane = lane - lax.broadcasted_iota(jnp.int32, (group, span), 0)
        mark = lane == seat_ref[:, :1] * group
        here_ref[...] = jnp.full(here_ref.shape, -1.0, F32)
        for q in range(count):
            said = row_ref[(q + 1) * size - 8 : (q + 1) * size, :span].astype(F32)
            said = said[:SIDE] * DIGIT + said[SIDE:]
            for k in range(SIDE):
                table = jnp.broadcast_to(said[k : k + 1], (group, span))
                label = jnp.sum(jnp.where(mark, table, 0.0), axis=1, keepdims=True) - 1.0
                if k < 2:
                    at = q * size + k * group
                    here_ref[at : at + group, :] = label
                else:
                    at = q * rest + (k - 2) * group
                    next_ref[at : at + group, :] = label

    fine_step(row_ref, weight_ref, grad_ref, total_ref, here_ref)

    @pl.when(pl.program_id(0) == steps - 1)
    def _():
        pair_ref[...] = total_ref[...].astype(BF16)


def fine_first(rows, weight, seat, wide_count, group, tile=512):
    count, width = rows.shape
    columns = weight.shape[2]
    steps = columns // tile
    after_rows = 2 * wide_count * group
    return call(
        functools.partial(fine_first_body, steps, wide_count, group),
        (steps,),
        [
            whole(rows),
            pl.BlockSpec((1, width, tile), lambda i: (0, 0, i)),
            whole(seat),
        ],
        (
            pl.BlockSpec((count, tile), lambda i: (0, i)),
            pl.BlockSpec((count, width), lambda i: (0, 0)),
            pl.BlockSpec((after_rows, 1), lambda i: (0, 0)),
        ),
        (
            jax.ShapeDtypeStruct((count, columns), BF16),
            jax.ShapeDtypeStruct((count, width), BF16),
            jax.ShapeDtypeStruct((after_rows, 1), F32),
        ),
        4 * count * width * columns,
        [pltpu.VMEM((count, width), F32), pltpu.VMEM((count, 1), F32)],
    )(rows, weight, seat)


def fine_second_body(
    steps, row_ref, weight_ref, label_ref, pair_ref, order_ref, token_ref, grad_ref, line_ref,
    total_ref, tile_ref,
):
    fine_step(row_ref, weight_ref, grad_ref, total_ref, label_ref)
    count, kept = order_ref.shape
    size, former = row_ref.shape[0] // count, pair_ref.shape[0] // count
    width = total_ref.shape[1]

    @pl.when(pl.program_id(0) == steps - 1)
    def _():
        pieces = width // 128
        split = kept // 2
        old = lax.broadcasted_iota(jnp.int32, (former, kept), 0)
        new = lax.broadcasted_iota(jnp.int32, (size, kept), 0)
        for q in range(count):
            order = order_ref[q : q + 1, :]
            pick = (old == jnp.where(order < split, order, -1)).astype(F32).astype(BF16)
            moved = dot(pick, pair_ref[q * former : (q + 1) * former, :], 0, 0)
            pick = (new == order - split).astype(F32).astype(BF16)
            rows = total_ref[q * size : (q + 1) * size, :].astype(BF16)
            moved = moved + dot(pick, rows, 0, 0)
            for j in range(pieces):
                tile_ref[pl.ds(j, kept, pieces), :] = moved[:, j * 128 : (j + 1) * 128]
            span = kept * pieces
            line_ref[q * span : (q + 1) * span, :] = tile_ref[...].astype(BF16)


def fine_second(rows, weight, labels, pairs, order, token, tile=512):
    count, width = rows.shape
    columns = weight.shape[2]
    steps = columns // tile
    kept = order.shape[1]
    lines = order.shape[0] * kept * (width // 128)
    return call(
        functools.partial(fine_second_body, steps),
        (steps,),
        [
            whole(rows),
            pl.BlockSpec((1, width, tile), lambda i: (0, 0, i)),
            whole(labels),
            whole(pairs),
            whole(order),
            whole(token),
        ],
        (
            pl.BlockSpec((count, tile), lambda i: (0, i)),
            pl.BlockSpec((lines, 128), lambda i: (0, 0)),
        ),
        (
            jax.ShapeDtypeStruct((count, columns), BF16),
            jax.ShapeDtypeStruct((lines, 128), BF16),
        ),
        4 * count * width * columns,
        [pltpu.VMEM((count, width), F32), pltpu.VMEM((kept * (width // 128), 128), F32)],
    )(rows, weight, labels, pairs, order, token)


def finish_body(own_ref, one_ref, two_ref, three_ref, slot_ref, back_ref, out_ref, line_ref):
    total = own_ref[0] + one_ref[...] + two_ref[...] + three_ref[...]
    rows, width = out_ref.shape
    pieces = width // 128
    count = back_ref.shape[0] // pieces
    line_ref[...] = back_ref[...].astype(F32)
    ids = lax.broadcasted_iota(jnp.int32, (rows, count), 1)
    slots = slot_ref[...]
    hit = slots[:, 0:1] == ids
    for k in range(1, slots.shape[1]):
        hit = hit | (slots[:, k : k + 1] == ids)
    pick = hit.astype(F32).astype(BF16)
    for j in range(pieces):
        part = line_ref[pl.ds(j, count, pieces), :].astype(BF16)
        span = slice(j * 128, (j + 1) * 128)
        out_ref[:, span] = total[:, span] + dot(pick, part, 1, 0)


def finish(own, tails, slots, back):
    inputs = [own, *tails, slots, back]
    return call(
        finish_body,
        (1,),
        [pl.BlockSpec((1, *own.shape[1:]), lambda i: (0, 0, 0))] + [whole(a) for a in inputs[1:]],
        whole(tails[0]),
        jax.ShapeDtypeStruct(tails[0].shape, F32),
        2 * own.shape[1] * back.size,
        [pltpu.VMEM(back.shape, F32)],
    )(*inputs)


def outer_body(parts, moment, token_ref, *refs):
    lefts, rights = refs[:parts], refs[parts : 2 * parts]
    left_ref, right_ref = refs[-2:]
    out_ref = refs[-3]
    edge = 0
    for left in lefts:
        left_ref[edge : edge + left.shape[0], :] = left[...]
        edge += left.shape[0]

    @pl.when(pl.program_id(0) == 0)
    def _():
        edge = 0
        for right in rights:
            right_ref[edge : edge + right.shape[0], :] = right[...]
            edge += right.shape[0]

    total = dot(left_ref[...], right_ref[...], 0, 0)
    if moment:
        out_ref[0] = BETA * refs[2 * parts][0] + total
    else:
        out_ref[...] = total.astype(out_ref.dtype)


def outer(token, lefts, rights, moment=None, tile=256):
    width, columns = lefts[0].shape[1], rights[0].shape[1]
    depth = sum(a.shape[0] for a in lefts)
    in_specs = [whole(token)]
    in_specs += [pl.BlockSpec((a.shape[0], tile), lambda i: (0, i)) for a in lefts]
    in_specs += [whole(b) for b in rights]
    inputs = [token, *lefts, *rights]
    if moment is None:
        out_spec = pl.BlockSpec((tile, columns), lambda i: (i, 0))
        out = jax.ShapeDtypeStruct((width, columns), BF16)
    else:
        out_spec = pl.BlockSpec((1, tile, columns), lambda i: (0, i, 0))
        in_specs.append(out_spec)
        inputs.append(moment)
        out = jax.ShapeDtypeStruct((1, width, columns), F32)
    return call(
        functools.partial(outer_body, len(lefts), moment is not None),
        (width // tile,),
        in_specs,
        out_spec,
        out,
        2 * width * columns * depth,
        [pltpu.VMEM((depth, tile), BF16), pltpu.VMEM((depth, columns), BF16)],
    )(*inputs)


def ordered_outer_body(parts, half, order_ref, token_ref, *refs):
    del order_ref, token_ref
    lefts, rights = refs[: 2 * parts], refs[2 * parts : 3 * parts]
    give_ref, keep_ref, left_ref, right_ref = refs[3 * parts :]
    step = pl.program_id(0)
    edge = 0
    for k in range(parts):
        rows, wide = lefts[2 * k].shape
        left_ref[edge : edge + rows, :wide] = lefts[2 * k][...]
        left_ref[edge : edge + rows, wide:] = lefts[2 * k + 1][...]
        edge += rows

    @pl.when(step == 0)
    def _():
        edge = 0
        for right in rights:
            right_ref[edge : edge + right.shape[0], :] = right[...]
            edge += right.shape[0]

    total = dot(left_ref[...], right_ref[...], 0, 0)

    @pl.when(step < half)
    def _():
        give_ref[...] = total

    @pl.when(step >= half)
    def _():
        keep_ref[...] = total


def ordered_outer(order, token, lefts, rights):
    width, columns = lefts[0].shape[1], rights[0].shape[1]
    depth = sum(a.shape[0] for a in lefts)
    tile = width // order.shape[0]
    steps = order.shape[0] // 2
    half = steps // 2
    in_specs = [pl.BlockSpec(token.shape, lambda i, o: (0, 0))]
    inputs = [token]
    for a in lefts:
        in_specs.append(pl.BlockSpec((a.shape[0], tile), lambda i, o: (0, o[2 * i])))
        in_specs.append(pl.BlockSpec((a.shape[0], tile), lambda i, o: (0, o[2 * i + 1])))
        inputs += [a, a]
    in_specs += [pl.BlockSpec(b.shape, lambda i, o: (0, 0)) for b in rights]
    out = jax.ShapeDtypeStruct((width // 2, columns), F32)
    return pl.pallas_call(
        functools.partial(ordered_outer_body, len(lefts), half),
        name="ordered_outer",
        grid_spec=pltpu.PrefetchScalarGridSpec(
            num_scalar_prefetch=1,
            grid=(steps,),
            in_specs=in_specs,
            out_specs=(
                pl.BlockSpec((2 * tile, columns), lambda i, o: (jnp.minimum(i, half - 1), 0)),
                pl.BlockSpec((2 * tile, columns), lambda i, o: (jnp.maximum(i - half, 0), 0)),
            ),
            scratch_shapes=[pltpu.VMEM((depth, 2 * tile), BF16), pltpu.VMEM((depth, columns), BF16)],
        ),
        out_shape=stored((out, out)),
        compiler_params=pltpu.CompilerParams(vmem_limit_bytes=48 << 20),
        cost_estimate=pl.CostEstimate(
            flops=2 * depth * width * columns, transcendentals=0, bytes_accessed=1 << 24
        ),
    )(order, *inputs, *rights)


def step(
    samples, clusters, blocks, labels, coarse_weight, coarse_moment, fine_weight, fine_moment
):
    rows_here, width = samples.shape
    wide_count = lax.axis_size("wide")
    narrow_count = lax.axis_size("narrow")
    picked = blocks.shape[1]
    top = clusters.shape[1]
    owners = wide_count * narrow_count
    capacity = 5 * rows_here * picked // (4 * owners)
    columns = coarse_weight.shape[1]
    narrow_at = lax.axis_index("narrow")
    wide_at = lax.axis_index("wide")
    column_ids = narrow_at * columns + jnp.arange(columns, dtype=jnp.int32)
    column_ids = column_ids[None, :].astype(F32)
    per_chunk = SIDE * capacity
    kept = SIDE * per_chunk

    line = [samples] + [send(samples, first_line(s)) for s in STEPS[1:]]
    line = jnp.concatenate(line, axis=0)
    filler = jnp.full((8 - top, rows_here), -1, jnp.int32)
    notes = jnp.concatenate([blocks.T, labels.T, clusters.T, filler], axis=0)
    note_line = jnp.stack([notes] + [send(notes, first_line(s)) for s in STEPS[1:]])
    note_chunks = [note_line] + [send(note_line, second_line(s)) for s in STEPS[1:]]
    near = [send(line, second_line(s)) for s in STEPS[1:3]]
    rows = [line, *near, None]
    before = (jnp.arange(rows_here)[:, None] < jnp.arange(rows_here)[None, :]).astype(BF16)

    places = jnp.arange(kept, dtype=jnp.int32)
    source_x, source_z = places // capacity // SIDE, places // capacity % SIDE
    step_x = (narrow_at // SIDE - source_x) % SIDE
    step_z = (narrow_at % SIDE - source_z) % SIDE
    turn = jnp.array([STEPS.index(s) for s in (0, 1, 2, -1)], dtype=jnp.int32)
    turn_x = sum(jnp.where(step_x == s, turn[s], 0) for s in range(SIDE))
    turn_z = sum(jnp.where(step_z == s, turn[s], 0) for s in range(SIDE))
    order_0 = turn_x * per_chunk + turn_z * capacity + places % capacity
    order_1 = turn_z * per_chunk + turn_x * capacity + places % capacity
    order = jnp.stack([order_0, order_1] * (wide_count // 2))

    grads, parts = [None] * SIDE, [None] * SIDE

    def coarse_of(k, *earlier):
        grads[k], parts[k] = coarse(
            rows[k],
            coarse_weight,
            note_chunks[k],
            after(column_ids, *earlier),
            top,
            F32 if k == 0 else BF16,
        )
        return parts[k]

    def compact_of(k, message, length, *earlier):
        place = after(slots[k], *earlier) if earlier else slots[k]
        return compact(rows[k], place, message, k % 2, per_chunk, length)

    mine = jnp.arange(wide_count, dtype=jnp.int32) * narrow_count + narrow_at
    mine = jnp.broadcast_to(mine[:, None], (wide_count, rows_here))
    done = coarse_of(0)
    rows[3] = send(after(line, done, *near), second_line(STEPS[3]))
    slots, spare = prepare(after(mine, done), note_chunks, picked, capacity, width)
    half = 2 * per_chunk
    message = stamp(spare, wide_count, half)
    message = compact_of(0, message, half + 8)
    message = compact_of(1, message, half + 8)
    got_1 = swap_wide(message)
    coarse_of(1, message)
    coarse_of(2, parts[1])
    message = compact_of(2, None, half, parts[2])
    message = compact_of(3, message, half)
    got_2 = swap_wide(message)
    coarse_of(3, message)
    shares = []
    for k in (1, 2, 3):
        shares.append(send(after(parts[k], message), second_line(-STEPS[k])).astype(F32))

    y_at, core_at = wide_at // 2, wide_at % 2
    order_y = (y_at + jnp.array(STEPS, dtype=jnp.int32)) % SIDE
    blocks_order = jnp.concatenate([order_y * 2 + 1 - core_at, order_y * 2 + core_at])
    give, keep = ordered_outer(blocks_order, after(column_ids, parts[3]), rows, grads)
    given = send(give, partner_map())
    got_1, got_2 = got_1.reshape(-1, width), got_2.reshape(-1, width)
    seat = jnp.full((1, 128), wide_at, jnp.int32)
    grad_1, pair_1, label_2 = fine_first(
        got_1, fine_weight, after(seat, keep), wide_count, per_chunk
    )
    chip_sum = after(keep, pair_1) + given
    chip_sum = chip_sum.reshape(SIDE, width // wide_count, columns)
    pieces = [send(chip_sum[j].astype(BF16), column_map(STEPS[j])) for j in (1, 2, 3)]
    total = after(parts[0], pair_1)
    for share in shares:
        total = total + share
    total = total.reshape(SIDE, rows_here, width)
    tails = [send(total[j], first_line(-STEPS[j])) for j in (1, 2, 3)]
    grad_2, pairs = fine_second(
        got_2, fine_weight, label_2, pair_1, order, after(column_ids, total, chip_sum)
    )
    pairs = pairs.reshape(owners, -1, 128)
    back = lax.all_to_all(pairs, AXES, split_axis=0, concat_axis=0, tiled=True)

    new_coarse = BETA * after(coarse_moment, pairs) + chip_sum[0]
    for piece in pieces:
        new_coarse = new_coarse + piece.astype(F32)
    blocks = after(blocks, pairs)
    every = jnp.arange(owners, dtype=jnp.int32)
    own_hit = jnp.any(blocks.T[None] == every[:, None, None], axis=1)
    own_place = jnp.dot(own_hit.astype(BF16), before, preferred_element_type=F32)
    own_place = own_place.T.astype(jnp.int32)
    own_slots = blocks * capacity + jnp.sum(
        jnp.where(blocks[:, :, None] == every[None, None, :], own_place[:, None, :], 0), axis=2
    )

    new_fine = outer(
        after(column_ids, pairs), [got_1, got_2], [grad_1, grad_2], fine_moment
    )
    result = finish(total, tails, own_slots, back.reshape(-1, 128))
    return (result, new_coarse, new_fine)


def solution(mesh):
    in_specs = (
        P(("wide", "narrow"), None),
        P(("wide", "narrow"), None),
        P(("wide", "narrow"), None),
        P(("wide", "narrow"), None),
        P(None, "narrow"),
        P("wide", "narrow"),
        P(("wide", "narrow"), None, None),
        P(("wide", "narrow"), None, None),
    )
    out_specs = (
        P(("wide", "narrow"), None),
        P("wide", "narrow"),
        P(("wide", "narrow"), None, None),
    )
    return jax.shard_map(step, mesh=mesh, in_specs=in_specs, out_specs=out_specs, check_vma=False)
```

profile of v0, /device:TPU:32, one launch (start us, length us, event | category | flops | bytes accessed | tf_op | source)
XLA Modules:
  0.0 191.1 jit_solution(13528216417790436612)
XLA Ops:
  2.8 3.0 %collective-permute-start.2 = (bf16[128,1024]{1,0:T(8,128)(2,1)}, bf16[128,1024]{1,0:T(8,128)(2,1)S(1)}, u32[]{:S(2)}, u32[]{:S(2)}) collective-permute-start(bf16[128,1024]{1,0:T(8,128)(2,1)} %param.10), channel_id=1, source_target_pairs={{0,2},{1,3},{2,0},{3,1},{4,6},{5,7},{6,4},{7,5},{8,10},{9,11},{10,... | collective-permute-start | bytes 786440 | tf_op jit(solution)/shard_map/ppermute | solution.py:48
  9.3 3.8 %collective-permute-done.2 = bf16[128,1024]{1,0:T(8,128)(2,1)S(1)} collective-permute-done((bf16[128,1024]{1,0:T(8,128)(2,1)}, bf16[128,1024]{1,0:T(8,128)(2,1)S(1)}, u32[]{:S(2)}, u32[]{:S(2)}) %collective-permute-start.2) | collective-permute-done | bytes 262176 | tf_op jit(solution)/shard_map/ppermute | solution.py:48
  13.1 2.8 %collective-permute-start.10 = (bf16[512,1024]{1,0:T(8,128)(2,1)S(1)}, bf16[512,1024]{1,0:T(8,128)(2,1)S(1)}, u32[]{:S(2)}, u32[]{:S(2)}) collective-permute-start(bf16[512,1024]{1,0:T(8,128)(2,1)S(1)} %constant_dynamic-update-slice_fusion.row_ref.refs_0_.refs_1_), channel_id=1, source_target_pairs={{0,12},{1,13},{2,14},{3,15},{4,0},{5,1},{6,2},{7,3},{8,4},{9,5},{1... | collective-permute-start | bytes 3145736 | tf_op jit(solution)/shard_map/ppermute | solution.py:48
  20.8 2.7 %collective-permute-done.5 = s32[24,128]{1,0:T(8,128)S(1)} collective-permute-done((s32[24,128]{1,0:T(8,128)S(1)}, s32[24,128]{1,0:T(8,128)S(1)}, u32[]{:S(2)}, u32[]{:S(2)}) %collective-permute-start.5) | collective-permute-done | bytes 12320 | tf_op jit(solution)/shard_map/ppermute | solution.py:48
  29.5 5.2 %shard_map.121 = (bf16[512,1024]{1,0:T(8,128)(2,1)}, f32[512,1024]{1,0:T(8,128)}) custom-call(bf16[512,1024]{1,0:T(8,128)(2,1)S(1)} %constant_dynamic-update-slice_fusion.row_ref.refs_0_.refs_1_, bf16[1024,1024]{1,0:T(8,128)(2,1)S(1)} %copy-done.15, s32[4,24,128]{2,1,0:T(8,128)S(1)} %pad_add_fusion.note_ref.refs_0_, ...), custom_call_target="tpu_custom_call" | custom-call | flops 2147483648 | bytes 2147483 | tf_op jit(solution)/shard_map/pallas_call | solution.py:239
  44.5 4.5 %all-to-all-start = ((bf16[8,88,1024]{2,1,0:T(8,128)(2,1)}), bf16[8,88,1024]{2,1,0:T(8,128)(2,1)S(1)}, u32[]{:S(2)}, u32[]{:S(2)}) async-start(bf16[8,88,1024]{2,1,0:T(8,128)(2,1)} %shard_map.125), calls=%async_computation | async-start | bytes 2883584 | tf_op jit(solution)/shard_map/all_to_all | solution.py:56
  56.0 4.9 %shard_map.126 = (bf16[512,1024]{1,0:T(8,128)(2,1)}, bf16[512,1024]{1,0:T(8,128)(2,1)}) custom-call(bf16[512,1024]{1,0:T(8,128)(2,1)S(1)} %copy-done.5, bf16[1024,1024]{1,0:T(8,128)(2,1)S(1)} %copy-done.16, s32[4,24,128]{2,1,0:T(8,128)S(1)} %copy-done.23, f32[1,1024]{1,0:T(1,128)S(1)} %copy-done.10), custom_call_target="tpu_custom_call" | custom-call | flops 2147483648 | bytes 2147483 | tf_op jit(solution)/shard_map/pallas_call | solution.py:239
  60.9 5.0 %shard_map.127 = (bf16[512,1024]{1,0:T(8,128)(2,1)}, bf16[512,1024]{1,0:T(8,128)(2,1)}) custom-call(bf16[512,1024]{1,0:T(8,128)(2,1)S(1)} %copy-done.2, bf16[1024,1024]{1,0:T(8,128)(2,1)S(1)} %copy-done.16, s32[4,24,128]{2,1,0:T(8,128)S(1)} %copy-done.21, f32[1,1024]{1,0:T(1,128)S(1)} %copy-done.10), custom_call_target="tpu_custom_call" | custom-call | flops 2147483648 | bytes 2147483 | tf_op jit(solution)/shard_map/pallas_call | solution.py:239
  68.7 2.6 %collective-permute-start.12 = (bf16[512,1024]{1,0:T(8,128)(2,1)}, bf16[512,1024]{1,0:T(8,128)(2,1)}, u32[]{:S(2)}, u32[]{:S(2)}) collective-permute-start(bf16[512,1024]{1,0:T(8,128)(2,1)} %get-tuple-element.58), channel_id=1, source_target_pairs={{0,12},{1,13},{2,14},{3,15},{4,0},{5,1},{6,2},{7,3},{8,4},{9,5},{1... | collective-permute-start | bytes 3145736 | tf_op jit(solution)/shard_map/ppermute | solution.py:48
  71.3 4.9 %shard_map.130 = (bf16[512,1024]{1,0:T(8,128)(2,1)}, bf16[512,1024]{1,0:T(8,128)(2,1)}) custom-call(bf16[512,1024]{1,0:T(8,128)(2,1)S(1)} %collective-permute-done.11.row_ref.refs_6_.refs_7_, bf16[1024,1024]{1,0:T(8,128)(2,1)S(1)} %copy-done.17, s32[4,24,128]{2,1,0:T(8,128)S(1)} %copy-done.19, f32[1,1024]{1,0:T(1,128)S(1)} %copy-done.11), custom_call_target="tpu_custom_call" | custom-call | flops 2147483648 | bytes 2147483 | tf_op jit(solution)/shard_map/pallas_call | solution.py:239
  77.8 5.3 %all-to-all-start.1 = ((bf16[8,80,1024]{2,1,0:T(8,128)(2,1)}), bf16[8,80,1024]{2,1,0:T(8,128)(2,1)}, u32[]{:S(2)}, u32[]{:S(2)}) async-start(bf16[8,80,1024]{2,1,0:T(8,128)(2,1)} %shard_map.129), calls=%async_computation.1 | async-start | bytes 2621440 | tf_op jit(solution)/shard_map/all_to_all | solution.py:56
  86.8 11.7 %ordered_outer.1 = (f32[512,1024]{1,0:T(8,128)}, f32[512,1024]{1,0:T(8,128)}) custom-call(s32[8]{0:T(128)S(1)} %pad_add_fusion.1.order_ref, f32[1,1024]{1,0:T(1,128)S(1)} %copy-done.12, bf16[512,1024]{1,0:T(8,128)(2,1)S(1)} %constant_dynamic-update-slice_fusion.row_ref.refs_0_.refs_1_, ...), custom_call_target="tpu_custom_call" | custom-call | flops 4294967296 | bytes 16777216 | tf_op jit(solution)/shard_map/ordered_outer/pallas_call | solution.py:525
  99.0 11.0 %shard_map.131 = (bf16[704,2048]{1,0:T(8,128)(2,1)}, bf16[704,1024]{1,0:T(8,128)(2,1)}, f32[640,1]{1,0:T(8,128)}) custom-call(bf16[704,1024]{1,0:T(8,128)(2,1)S(1)} %bitcast.24, bf16[1,1024,2048]{2,1,0:T(8,128)(2,1)S(1)} %copy-done.14, s32[1,128]{1,0:T(1,128)S(1)} %broadcast_in_dim.60.seat_ref), custom_call_target="tpu_custom_call" | custom-call | flops 5905580032 | bytes 5905580 | tf_op jit(solution)/shard_map/pallas_call | solution.py:320
  110.1 2.6 %convert_add_fusion = f32[512,1024]{1,0:T(8,128)S(1)} fusion(bf16[512,1024]{1,0:T(8,128)(2,1)} %collective-permute-done.14, bf16[512,1024]{1,0:T(8,128)(2,1)} %collective-permute-done.13, f32[512,1024]{1,0:T(8,128)S(1)} %copy-done.27, bf16[512,1024]{1,0:T(8,128)(2,1)} %collective-permute-done.12), kind=kLoop, calls=%fused_computation | loop fusion | flops 3145728 | bytes 7340032 | tf_op jit(solution)/shard_map/add | solution.py:637
  115.0 13.2 %shard_map.132 = (bf16[640,2048]{1,0:T(8,128)(2,1)}, bf16[10240,128]{1,0:T(8,128)(2,1)}) custom-call(bf16[640,1024]{1,0:T(8,128)(2,1)} %bitcast.13.row_ref.refs_1_, bf16[1,1024,2048]{2,1,0:T(8,128)(2,1)} %weight_ref.11, f32[640,1]{1,0:T(8,128)S(1)} %copy-done.26, bf16[704,1024]{1,0:T(8,128)(2,1)S(1)} %copy-done.25, s32[8,160]{1,0:T(8,128)S(1)} %copy-done.13, ...), custom_call_target="tpu_custom_call" | custom-call | flops 5368709120 | bytes 5368709 | tf_op jit(solution)/shard_map/pallas_call | solution.py:377
  128.3 9.2 %all-to-all-start.2 = ((bf16[128,80,128]{2,1,0:T(8,128)(2,1)}), bf16[128,80,128]{2,1,0:T(8,128)(2,1)}, u32[]{:S(2)}, u32[]{:S(2)}) async-start(bf16[128,80,128]{2,1,0:T(8,128)(2,1)} %bitcast.26), calls=%async_computation.2 | async-start | bytes 5242880 | tf_op jit(solution)/shard_map/all_to_all | solution.py:644
  138.6 2.6 %collective-permute-start.17 = (f32[128,1024]{1,0:T(8,128)}, f32[128,1024]{1,0:T(8,128)}, u32[]{:S(2)}, u32[]{:S(2)}) collective-permute-start(f32[128,1024]{1,0:T(8,128)} %get-tuple-element.75), channel_id=1, source_target_pairs={{0,2},{1,3},{2,0},{3,1},{4,6},{5,7},{6,4},{7,5},{8,10},{9,11},{10,... | collective-permute-start | bytes 1572872 | tf_op jit(solution)/shard_map/ppermute | solution.py:48
  143.3 12.7 %shard_map.134 = f32[1,1024,2048]{2,1,0:T(8,128)} custom-call(f32[1,1024]{1,0:T(1,128)S(1)} %copy-done.12, bf16[704,1024]{1,0:T(8,128)(2,1)S(1)} %bitcast.25, bf16[640,1024]{1,0:T(8,128)(2,1)} %bitcast.13.row_ref.refs_1_, bf16[704,2048]{1,0:T(8,128)(2,1)} %get-tuple-element.69.refs_2_, bf16[640,2048]{1,0:T(8,128)(2,1)S(1)} %copy-done, f32[1,1024,2048]{2,1,0:T(8,128)} %refs_4_.1), custom_call_target="tpu_custom_call" | custom-call | flops 5637144576 | bytes 5637144 | tf_op jit(solution)/shard_map/pallas_call | solution.py:470
  156.0 3.5 %fusion.16 = (bf16[512,1024]{1,0:T(8,128)(2,1)S(1)}, f32[512,1024]{1,0:T(8,128)}) fusion(f32[512,1024]{1,0:T(8,128)S(1)} %copy-done.28, f32[512,1024]{1,0:T(8,128)} %collective-permute-done.18), kind=kLoop, calls=%fused_computation.65 | loop fusion | flops 1048576 | bytes 7340032 | tf_op jit(solution)/shard_map/convert.2
  162.2 2.9 %collective-permute-start.21 = (bf16[128,1024]{1,0:T(8,128)(2,1)}, bf16[128,1024]{1,0:T(8,128)(2,1)S(1)}, u32[]{:S(2)}, u32[]{:S(2)}) collective-permute-start(bf16[128,1024]{1,0:T(8,128)(2,1)} %get-tuple-element.79), channel_id=1, source_target_pairs={{0,64},{1,65},{2,66},{3,67},{4,68},{5,69},{6,70},{7,71},{8,72},{9,... | collective-permute-start | bytes 786440 | tf_op jit(solution)/shard_map/ppermute | solution.py:48
  165.1 9.6 %collective-permute-done.19 = bf16[128,1024]{1,0:T(8,128)(2,1)S(1)} collective-permute-done((bf16[128,1024]{1,0:T(8,128)(2,1)S(1)}, bf16[128,1024]{1,0:T(8,128)(2,1)S(1)}, u32[]{:S(2)}, u32[]{:S(2)}) %collective-permute-start.19) | collective-permute-done | bytes 262176 | tf_op jit(solution)/shard_map/ppermute | solution.py:48
  176.5 3.2 %select_reduce_fusion = s32[128,8]{1,0:T(8,128)S(1)} fusion(s32[128,128]{1,0:T(8,128)S(1)} %convolution_convert_fusion, s32[128,8]{1,0:T(8,128)} %copy.22), kind=kLoop, calls=%fused_computation.6 | loop fusion | flops 392192 | bytes 73728 | tf_op jit(solution)/shard_map/reduce_sum | solution.py:654
  180.6 2.7 %collective-permute-done.20 = bf16[128,1024]{1,0:T(8,128)(2,1)S(1)} collective-permute-done((bf16[128,1024]{1,0:T(8,128)(2,1)}, bf16[128,1024]{1,0:T(8,128)(2,1)S(1)}, u32[]{:S(2)}, u32[]{:S(2)}) %collective-permute-start.20) | collective-permute-done | bytes 262176 | tf_op jit(solution)/shard_map/ppermute | solution.py:48
  185.3 5.8 %shard_map.133 = f32[128,1024]{1,0:T(8,128)} custom-call(f32[4,128,1024]{2,1,0:T(8,128)S(1)} %bitcast.23, f32[128,1024]{1,0:T(8,128)} %collective-permute-done.15.one_ref, f32[128,1024]{1,0:T(8,128)} %collective-permute-done.16.two_ref, f32[128,1024]{1,0:T(8,128)} %collective-permute-done.17.three_ref, s32[128,8]{1,0:T(8,128)S(1)} %add.320.slot_ref, ...), custom_call_target="tpu_custom_call" | custom-call | flops 335544320 | bytes 335544 | tf_op jit(solution)/shard_map/pallas_call | solution.py:421
  (139 shorter events, 54.6 us)
Async XLA Ops:
  0.7 6.7 %collective-permute-start = (bf16[128,1024]{1,0:T(8,128)(2,1)}, bf16[128,1024]{1,0:T(8,128)(2,1)S(1)}, u32[]{:S(2)}, u32[]{:S(2)}) collective-permute-start(bf16[128,1024]{1,0:T(8,128)(2,1)} %param.10), channel_id=1, source_target_pairs={{0,1},{1,2},{2,3},{3,0},{4,5},{5,6},{6,7},{7,4},{8,9},{9,10},{10,1... | collective-permute-start | bytes 786440 | tf_op jit(solution)/shard_map/ppermute | solution.py:48
  2.6 6.6 %collective-permute-start.1 = (bf16[128,1024]{1,0:T(8,128)(2,1)}, bf16[128,1024]{1,0:T(8,128)(2,1)S(1)}, u32[]{:S(2)}, u32[]{:S(2)}) collective-permute-start(bf16[128,1024]{1,0:T(8,128)(2,1)} %param.10), channel_id=1, source_target_pairs={{0,3},{1,0},{2,1},{3,2},{4,7},{5,4},{6,5},{7,6},{8,11},{9,8},{10,9... | collective-permute-start | bytes 786440 | tf_op jit(solution)/shard_map/ppermute | solution.py:48
  2.8 10.3 %collective-permute-start.2 = (bf16[128,1024]{1,0:T(8,128)(2,1)}, bf16[128,1024]{1,0:T(8,128)(2,1)S(1)}, u32[]{:S(2)}, u32[]{:S(2)}) collective-permute-start(bf16[128,1024]{1,0:T(8,128)(2,1)} %param.10), channel_id=1, source_target_pairs={{0,2},{1,3},{2,0},{3,1},{4,6},{5,7},{6,4},{7,5},{8,10},{9,11},{10,... | collective-permute-start | bytes 786440 | tf_op jit(solution)/shard_map/ppermute | solution.py:48
  13.1 25.8 %collective-permute-start.10 = (bf16[512,1024]{1,0:T(8,128)(2,1)S(1)}, bf16[512,1024]{1,0:T(8,128)(2,1)S(1)}, u32[]{:S(2)}, u32[]{:S(2)}) collective-permute-start(bf16[512,1024]{1,0:T(8,128)(2,1)S(1)} %constant_dynamic-update-slice_fusion.row_ref.refs_0_.refs_1_), channel_id=1, source_target_pairs={{0,12},{1,13},{2,14},{3,15},{4,0},{5,1},{6,2},{7,3},{8,4},{9,5},{1... | collective-permute-start | bytes 3145736 | tf_op jit(solution)/shard_map/ppermute | solution.py:48
  15.9 23.9 %collective-permute-start.6 = (bf16[512,1024]{1,0:T(8,128)(2,1)S(1)}, bf16[512,1024]{1,0:T(8,128)(2,1)S(1)}, u32[]{:S(2)}, u32[]{:S(2)}) collective-permute-start(bf16[512,1024]{1,0:T(8,128)(2,1)S(1)} %constant_dynamic-update-slice_fusion.row_ref.refs_0_.refs_1_), channel_id=1, source_target_pairs={{0,4},{1,5},{2,6},{3,7},{4,8},{5,9},{6,10},{7,11},{8,12},{9,13},{1... | collective-permute-start | bytes 3145736 | tf_op jit(solution)/shard_map/ppermute | solution.py:48
  16.1 4.6 %collective-permute-start.4 = (s32[24,128]{1,0:T(8,128)S(1)}, s32[24,128]{1,0:T(8,128)S(1)}, u32[]{:S(2)}, u32[]{:S(2)}) collective-permute-start(s32[24,128]{1,0:T(8,128)S(1)} %get-tuple-element.86), channel_id=1, source_target_pairs={{0,3},{1,0},{2,1},{3,2},{4,7},{5,4},{6,5},{7,6},{8,11},{9,8},{10,9... | collective-permute-start | bytes 36872 | tf_op jit(solution)/shard_map/ppermute | solution.py:48
  18.1 5.3 %collective-permute-start.5 = (s32[24,128]{1,0:T(8,128)S(1)}, s32[24,128]{1,0:T(8,128)S(1)}, u32[]{:S(2)}, u32[]{:S(2)}) collective-permute-start(s32[24,128]{1,0:T(8,128)S(1)} %get-tuple-element.86), channel_id=1, source_target_pairs={{0,2},{1,3},{2,0},{3,1},{4,6},{5,7},{6,4},{7,5},{8,10},{9,11},{10,... | collective-permute-start | bytes 36872 | tf_op jit(solution)/shard_map/ppermute | solution.py:48
  23.5 11.3 %collective-permute-start.9 = (s32[4,24,128]{2,1,0:T(8,128)S(1)}, s32[4,24,128]{2,1,0:T(8,128)S(1)}, u32[]{:S(2)}, u32[]{:S(2)}) collective-permute-start(s32[4,24,128]{2,1,0:T(8,128)S(1)} %pad_add_fusion.note_ref.refs_0_), channel_id=1, source_target_pairs={{0,8},{1,9},{2,10},{3,11},{4,12},{5,13},{6,14},{7,15},{8,0},{9,1},... | collective-permute-start | bytes 147464 | tf_op jit(solution)/shard_map/ppermute | solution.py:48
  25.9 8.9 %collective-permute-start.8 = (s32[4,24,128]{2,1,0:T(8,128)S(1)}, s32[4,24,128]{2,1,0:T(8,128)S(1)}, u32[]{:S(2)}, u32[]{:S(2)}) collective-permute-start(s32[4,24,128]{2,1,0:T(8,128)S(1)} %pad_add_fusion.note_ref.refs_0_), channel_id=1, source_target_pairs={{0,12},{1,13},{2,14},{3,15},{4,0},{5,1},{6,2},{7,3},{8,4},{9,5},{1... | collective-permute-start | bytes 147464 | tf_op jit(solution)/shard_map/ppermute | solution.py:48
  26.9 7.9 %collective-permute-start.7 = (s32[4,24,128]{2,1,0:T(8,128)S(1)}, s32[4,24,128]{2,1,0:T(8,128)S(1)}, u32[]{:S(2)}, u32[]{:S(2)}) collective-permute-start(s32[4,24,128]{2,1,0:T(8,128)S(1)} %pad_add_fusion.note_ref.refs_0_), channel_id=1, source_target_pairs={{0,4},{1,5},{2,6},{3,7},{4,8},{5,9},{6,10},{7,11},{8,12},{9,13},{1... | collective-permute-start | bytes 147464 | tf_op jit(solution)/shard_map/ppermute | solution.py:48
  39.9 27.4 %collective-permute-start.11 = (bf16[512,1024]{1,0:T(8,128)(2,1)S(1)}, bf16[512,1024]{1,0:T(8,128)(2,1)S(1)}, u32[]{:S(2)}, u32[]{:S(2)}) collective-permute-start(bf16[512,1024]{1,0:T(8,128)(2,1)S(1)} %constant_dynamic-update-slice_fusion.row_ref.refs_0_.refs_1_), channel_id=1, source_target_pairs={{0,8},{1,9},{2,10},{3,11},{4,12},{5,13},{6,14},{7,15},{8,0},{9,1},... | collective-permute-start | bytes 3145736 | tf_op jit(solution)/shard_map/ppermute | solution.py:48
  44.5 33.3 %all-to-all-start = ((bf16[8,88,1024]{2,1,0:T(8,128)(2,1)}), bf16[8,88,1024]{2,1,0:T(8,128)(2,1)S(1)}, u32[]{:S(2)}, u32[]{:S(2)}) async-start(bf16[8,88,1024]{2,1,0:T(8,128)(2,1)} %shard_map.125), calls=%async_computation | async-start | bytes 2883584 | tf_op jit(solution)/shard_map/all_to_all | solution.py:56
  68.7 41.4 %collective-permute-start.12 = (bf16[512,1024]{1,0:T(8,128)(2,1)}, bf16[512,1024]{1,0:T(8,128)(2,1)}, u32[]{:S(2)}, u32[]{:S(2)}) collective-permute-start(bf16[512,1024]{1,0:T(8,128)(2,1)} %get-tuple-element.58), channel_id=1, source_target_pairs={{0,12},{1,13},{2,14},{3,15},{4,0},{5,1},{6,2},{7,3},{8,4},{9,5},{1... | collective-permute-start | bytes 3145736 | tf_op jit(solution)/shard_map/ppermute | solution.py:48
  71.3 38.7 %collective-permute-start.13 = (bf16[512,1024]{1,0:T(8,128)(2,1)}, bf16[512,1024]{1,0:T(8,128)(2,1)}, u32[]{:S(2)}, u32[]{:S(2)}) collective-permute-start(bf16[512,1024]{1,0:T(8,128)(2,1)} %get-tuple-element.59), channel_id=1, source_target_pairs={{0,4},{1,5},{2,6},{3,7},{4,8},{5,9},{6,10},{7,11},{8,12},{9,13},{1... | collective-permute-start | bytes 3145736 | tf_op jit(solution)/shard_map/ppermute | solution.py:48
  76.2 33.8 %collective-permute-start.14 = (bf16[512,1024]{1,0:T(8,128)(2,1)}, bf16[512,1024]{1,0:T(8,128)(2,1)}, u32[]{:S(2)}, u32[]{:S(2)}) collective-permute-start(bf16[512,1024]{1,0:T(8,128)(2,1)} %get-tuple-element.60), channel_id=1, source_target_pairs={{0,8},{1,9},{2,10},{3,11},{4,12},{5,13},{6,14},{7,15},{8,0},{9,1},... | collective-permute-start | bytes 3145736 | tf_op jit(solution)/shard_map/ppermute | solution.py:48
  77.8 34.9 %all-to-all-start.1 = ((bf16[8,80,1024]{2,1,0:T(8,128)(2,1)}), bf16[8,80,1024]{2,1,0:T(8,128)(2,1)}, u32[]{:S(2)}, u32[]{:S(2)}) async-start(bf16[8,80,1024]{2,1,0:T(8,128)(2,1)} %shard_map.129), calls=%async_computation.1 | async-start | bytes 2621440 | tf_op jit(solution)/shard_map/all_to_all | solution.py:56
  98.5 57.5 %collective-permute-start.18 = (f32[512,1024]{1,0:T(8,128)}, f32[512,1024]{1,0:T(8,128)}, u32[]{:S(2)}, u32[]{:S(2)}) collective-permute-start(f32[512,1024]{1,0:T(8,128)} %get-tuple-element.67), channel_id=1, source_target_pairs={{0,16},{1,17},{2,18},{3,19},{4,20},{5,21},{6,22},{7,23},{8,24},{9,... | collective-permute-start | bytes 6291464 | tf_op jit(solution)/shard_map/ppermute | solution.py:48
  128.3 57.1 %all-to-all-start.2 = ((bf16[128,80,128]{2,1,0:T(8,128)(2,1)}), bf16[128,80,128]{2,1,0:T(8,128)(2,1)}, u32[]{:S(2)}, u32[]{:S(2)}) async-start(bf16[128,80,128]{2,1,0:T(8,128)(2,1)} %bitcast.26), calls=%async_computation.2 | async-start | bytes 5242880 | tf_op jit(solution)/shard_map/all_to_all | solution.py:644
  138.6 46.7 %collective-permute-start.17 = (f32[128,1024]{1,0:T(8,128)}, f32[128,1024]{1,0:T(8,128)}, u32[]{:S(2)}, u32[]{:S(2)}) collective-permute-start(f32[128,1024]{1,0:T(8,128)} %get-tuple-element.75), channel_id=1, source_target_pairs={{0,2},{1,3},{2,0},{3,1},{4,6},{5,7},{6,4},{7,5},{8,10},{9,11},{10,... | collective-permute-start | bytes 1572872 | tf_op jit(solution)/shard_map/ppermute | solution.py:48
  141.3 44.1 %collective-permute-start.16 = (f32[128,1024]{1,0:T(8,128)}, f32[128,1024]{1,0:T(8,128)}, u32[]{:S(2)}, u32[]{:S(2)}) collective-permute-start(f32[128,1024]{1,0:T(8,128)} %get-tuple-element.76), channel_id=1, source_target_pairs={{0,1},{1,2},{2,3},{3,0},{4,5},{5,6},{6,7},{7,4},{8,9},{9,10},{10,1... | collective-permute-start | bytes 1572872 | tf_op jit(solution)/shard_map/ppermute | solution.py:48
  141.3 44.1 %collective-permute-start.15 = (f32[128,1024]{1,0:T(8,128)}, f32[128,1024]{1,0:T(8,128)}, u32[]{:S(2)}, u32[]{:S(2)}) collective-permute-start(f32[128,1024]{1,0:T(8,128)} %get-tuple-element.77), channel_id=1, source_target_pairs={{0,3},{1,0},{2,1},{3,2},{4,7},{5,4},{6,5},{7,6},{8,11},{9,8},{10,9... | collective-permute-start | bytes 1572872 | tf_op jit(solution)/shard_map/ppermute | solution.py:48
  160.3 14.4 %collective-permute-start.19 = (bf16[128,1024]{1,0:T(8,128)(2,1)S(1)}, bf16[128,1024]{1,0:T(8,128)(2,1)S(1)}, u32[]{:S(2)}, u32[]{:S(2)}) collective-permute-start(bf16[128,1024]{1,0:T(8,128)(2,1)S(1)} %get-tuple-element.78), channel_id=1, source_target_pairs={{0,32},{1,33},{2,34},{3,35},{4,36},{5,37},{6,38},{7,39},{8,40},{9,... | collective-permute-start | bytes 786440 | tf_op jit(solution)/shard_map/ppermute | solution.py:48
  162.2 18.4 %collective-permute-start.21 = (bf16[128,1024]{1,0:T(8,128)(2,1)}, bf16[128,1024]{1,0:T(8,128)(2,1)S(1)}, u32[]{:S(2)}, u32[]{:S(2)}) collective-permute-start(bf16[128,1024]{1,0:T(8,128)(2,1)} %get-tuple-element.79), channel_id=1, source_target_pairs={{0,64},{1,65},{2,66},{3,67},{4,68},{5,69},{6,70},{7,71},{8,72},{9,... | collective-permute-start | bytes 786440 | tf_op jit(solution)/shard_map/ppermute | solution.py:48
  174.8 8.5 %collective-permute-start.20 = (bf16[128,1024]{1,0:T(8,128)(2,1)}, bf16[128,1024]{1,0:T(8,128)(2,1)S(1)}, u32[]{:S(2)}, u32[]{:S(2)}) collective-permute-start(bf16[128,1024]{1,0:T(8,128)(2,1)} %get-tuple-element.80), channel_id=1, source_target_pairs={{0,96},{1,97},{2,98},{3,99},{4,100},{5,101},{6,102},{7,103},{8,104... | collective-permute-start | bytes 786440 | tf_op jit(solution)/shard_map/ppermute | solution.py:48
  (35 other events, 215.2 us)
where the time goes:
time: 192 us; the launch traced here: 191 us
  Pallas kernels  81.9 us (43%)
  starting transfers between devices  52.1 us (27%)
  waiting for transfers between devices  22.3 us (12%)
  local copies, waits for them, and re-layouts  20.6 us (11%)
  other arithmetic  13 us (7%)
    ppermute x22, starting transfers between devices, send(): return lax.ppermute(value, AXES, pairs)  33.2 us
    ppermute x22, waiting for transfers between devices, send(): return lax.ppermute(value, AXES, pairs)  22.3 us
    pallas_call x4, Pallas kernels, coarse(): call(functools.partial(coarse_body, steps, top), (steps,), [whole(rows),...  20 us
    unnamed x71, local copies, waits for them, and re-layouts  14.8 us
    pallas_call x1, Pallas kernels, fine_second(): call(functools.partial(fine_second_body, steps), (steps,), [whole(rows),...  13.2 us
    pallas_call x1, Pallas kernels, outer(): call(functools.partial(outer_body, len(lefts), moment is not None), (widt...  12.7 us
    pallas_call x1, Pallas kernels, ordered_outer(): pl.pallas_call(functools.partial(ordered_outer_body, len(lefts), half), n...  11.7 us
    pallas_call x1, Pallas kernels, fine_first(): call(functools.partial(fine_first_body, steps, wide_count, group), (steps...  11 us
  transfers between devices with their start and end apart: 25, of which 7 were waited for; matrix products, arithmetic and copies ran while one was open for 10% of the time, Pallas kernels for 40%

commit v1 on v0

--- a/solution.py
+++ b/solution.py
@@ -68,6 +68,10 @@
     if isinstance(shape, tuple):
         return tuple(stored(one) for one in shape)
     return pltpu.HBM(shape.shape, shape.dtype)
+
+
+def from_hbm(*arrays):
+    return [pltpu.with_memory_space_constraint(a, pltpu.HBM) for a in arrays]
 
 
 def call(body, grid, in_specs, out_specs, out_shape, flops, scratch=(), aliases=None):
@@ -117,11 +121,12 @@
         jax.ShapeDtypeStruct((count, total, width), BF16),
         2 * count * size * width * rows.shape[0],
         aliases={2: 0} if earlier else None,
-    )(rows, slots, *earlier)
+    )(*from_hbm(rows), slots, *earlier)
 
 
 def prepare_body(picked, capacity, mine_ref, *refs):
-    notes, (slot_ref, spare_ref) = refs[:-2], refs[-2:]
+    chunks = len(refs) // 2 - 1
+    notes, slot_refs, spare_ref, own_ref = refs[:chunks], refs[chunks:-2], refs[-2], refs[-1]
     sources, _, rows = notes[0].shape
     count = mine_ref.shape[0]
     mine = mine_ref[...]
@@ -141,6 +146,15 @@
     two = lax.broadcasted_iota(jnp.int32, (rows, rows), 1)
     before = (one < two).astype(F32).astype(BF16)
     places = dot(jnp.concatenate(hits, axis=0).astype(BF16), before, 1, 0)
+    owners = own_ref.shape[1]
+    owner = lax.broadcasted_iota(jnp.int32, (owners, rows), 0)
+    chose = [notes[0][0, k : k + 1, :] == owner for k in range(picked)]
+    hit = jnp.zeros((owners, rows), F32)
+    for same in chose:
+        hit = jnp.where(same, 1.0, hit)
+    seat = dot(hit.astype(BF16), before, 1, 0) + (owner * capacity).astype(F32)
+    for k, same in enumerate(chose):
+        own_ref[k : k + 1, :] = jnp.sum(jnp.where(same, seat, 0.0), axis=0, keepdims=True)
     spare_ref[...] = jnp.zeros(spare_ref.shape, spare_ref.dtype)
     size = sources * capacity
     for k in range(len(notes)):
@@ -148,11 +162,11 @@
             at = k * sources + j
             place = places[at * count : (at + 1) * count] + float(j * capacity)
             slot = jnp.where(hits[at] > 0.0, place, -1.0)
-            slot_ref[k, :, j * rows : (j + 1) * rows] = slot.astype(jnp.int32)
+            slot_refs[k][:, j * rows : (j + 1) * rows] = slot.astype(jnp.int32)
         tag = jnp.concatenate(tags[k * sources : (k + 1) * sources], axis=1)
         high = jnp.floor(tag * (1.0 / DIGIT))
         digits = jnp.concatenate([high, tag - high * DIGIT], axis=0).astype(BF16)
-        found = dot(digits, selection(slot_ref[k], size), 1, 1)
+        found = dot(digits, selection(slot_refs[k][...], size), 1, 1)
         owner = lax.broadcasted_iota(jnp.int32, found.shape, 0)
         owner = jnp.where(owner >= count, owner - count, owner)
         lane = lax.broadcasted_iota(jnp.int32, found.shape, 1) - owner * size
@@ -164,9 +178,11 @@
 
 def prepare(mine, notes, picked, capacity, width):
     sources, _, rows = notes[0].shape
+    one = jax.ShapeDtypeStruct((mine.shape[0], sources * rows), jnp.int32)
     out = (
-        jax.ShapeDtypeStruct((len(notes), mine.shape[0], sources * rows), jnp.int32),
+        *[one] * len(notes),
         jax.ShapeDtypeStruct((2 * len(notes), width), F32),
+        jax.ShapeDtypeStruct((picked, rows), F32),
     )
     inputs = [mine, *notes]
     return call(
@@ -218,6 +234,9 @@
     grad = jnp.where(target, grad - 1.0, grad).astype(BF16)
     grad_ref[...] = grad
     part = dot(grad, weight, 1, 1)
+    if steps == 1:
+        part_ref[...] = part.astype(part_ref.dtype)
+        return
 
     @pl.when(step == 0)
     def _():
@@ -232,7 +251,7 @@
         part_ref[...] = (total_ref[...] + part).astype(part_ref.dtype)
 
 
-def coarse(rows, weight, notes, ids, top, dtype, tile=512):
+def coarse(rows, weight, notes, ids, top, dtype, tile=1024):
     count, width = rows.shape
     columns = weight.shape[1]
     steps = columns // tile
@@ -312,7 +331,7 @@
         pair_ref[...] = total_ref[...].astype(BF16)
 
 
-def fine_first(rows, weight, seat, wide_count, group, tile=512):
+def fine_first(rows, weight, seat, wide_count, group, tile=1024):
     count, width = rows.shape
     columns = weight.shape[2]
     steps = columns // tile
@@ -337,7 +356,7 @@
         ),
         4 * count * width * columns,
         [pltpu.VMEM((count, width), F32), pltpu.VMEM((count, 1), F32)],
-    )(rows, weight, seat)
+    )(*from_hbm(rows, weight), seat)
 
 
 def fine_second_body(
@@ -395,17 +414,19 @@
         ),
         4 * count * width * columns,
         [pltpu.VMEM((count, width), F32), pltpu.VMEM((kept * (width // 128), 128), F32)],
-    )(rows, weight, labels, pairs, order, token)
+    )(*from_hbm(rows, weight, labels, pairs), order, token)
 
 
 def finish_body(own_ref, one_ref, two_ref, three_ref, slot_ref, back_ref, out_ref, line_ref):
-    total = own_ref[0] + one_ref[...] + two_ref[...] + three_ref[...]
+    total = own_ref[0]
+    for tail in (one_ref, two_ref, three_ref):
+        total = total + tail[...].astype(F32)
     rows, width = out_ref.shape
     pieces = width // 128
     count = back_ref.shape[0] // pieces
     line_ref[...] = back_ref[...].astype(F32)
     ids = lax.broadcasted_iota(jnp.int32, (rows, count), 1)
-    slots = slot_ref[...]
+    slots = slot_ref[...].T.astype(jnp.int32)
     hit = slots[:, 0:1] == ids
     for k in range(1, slots.shape[1]):
         hit = hit | (slots[:, k : k + 1] == ids)
@@ -475,7 +496,7 @@
         out,
         2 * width * columns * depth,
         [pltpu.VMEM((depth, tile), BF16), pltpu.VMEM((depth, columns), BF16)],
-    )(*inputs)
+    )(inputs[0], *from_hbm(*inputs[1:]))
 
 
 def ordered_outer_body(parts, half, order_ref, token_ref, *refs):
@@ -540,7 +561,7 @@
         cost_estimate=pl.CostEstimate(
             flops=2 * depth * width * columns, transcendentals=0, bytes_accessed=1 << 24
         ),
-    )(order, *inputs, *rights)
+    )(order, inputs[0], *from_hbm(*inputs[1:], *rights))
 
 
 def step(
@@ -569,7 +590,6 @@
     note_chunks = [note_line] + [send(note_line, second_line(s)) for s in STEPS[1:]]
     near = [send(line, second_line(s)) for s in STEPS[1:3]]
     rows = [line, *near, None]
-    before = (jnp.arange(rows_here)[:, None] < jnp.arange(rows_here)[None, :]).astype(BF16)
 
     places = jnp.arange(kept, dtype=jnp.int32)
     source_x, source_z = places // capacity // SIDE, places // capacity % SIDE
@@ -602,61 +622,52 @@
     mine = jnp.arange(wide_count, dtype=jnp.int32) * narrow_count + narrow_at
     mine = jnp.broadcast_to(mine[:, None], (wide_count, rows_here))
     done = coarse_of(0)
-    rows[3] = send(after(line, done, *near), second_line(STEPS[3]))
-    slots, spare = prepare(after(mine, done), note_chunks, picked, capacity, width)
+    *slots, spare, own_slots = prepare(after(mine, done), note_chunks, picked, capacity, width)
     half = 2 * per_chunk
     message = stamp(spare, wide_count, half)
     message = compact_of(0, message, half + 8)
+    rows[3] = send(after(line, message, *near), second_line(STEPS[3]))
     message = compact_of(1, message, half + 8)
     got_1 = swap_wide(message)
     coarse_of(1, message)
     coarse_of(2, parts[1])
     message = compact_of(2, None, half, parts[2])
     message = compact_of(3, message, half)
-    got_2 = swap_wide(message)
     coarse_of(3, message)
+    got_2 = swap_wide(after(message, parts[3]))
     shares = []
     for k in (1, 2, 3):
         shares.append(send(after(parts[k], message), second_line(-STEPS[k])).astype(F32))
 
+    got_1, got_2 = got_1.reshape(-1, width), got_2.reshape(-1, width)
+    seat = jnp.full((1, 128), wide_at, jnp.int32)
+    grad_1, pair_1, label_2 = fine_first(
+        got_1, fine_weight, after(seat, parts[3]), wide_count, per_chunk
+    )
+    grad_2, pairs = fine_second(
+        got_2, fine_weight, label_2, pair_1, order, after(column_ids, pair_1)
+    )
+    pairs = pairs.reshape(owners, -1, 128)
+    back = lax.all_to_all(pairs, AXES, split_axis=0, concat_axis=0, tiled=True)
+
     y_at, core_at = wide_at // 2, wide_at % 2
     order_y = (y_at + jnp.array(STEPS, dtype=jnp.int32)) % SIDE
     blocks_order = jnp.concatenate([order_y * 2 + 1 - core_at, order_y * 2 + core_at])
-    give, keep = ordered_outer(blocks_order, after(column_ids, parts[3]), rows, grads)
+    give, keep = ordered_outer(blocks_order, after(column_ids, pairs), rows, grads)
     given = send(give, partner_map())
-    got_1, got_2 = got_1.reshape(-1, width), got_2.reshape(-1, width)
-    seat = jnp.full((1, 128), wide_at, jnp.int32)
-    grad_1, pair_1, label_2 = fine_first(
-        got_1, fine_weight, after(seat, keep), wide_count, per_chunk
-    )
-    chip_sum = after(keep, pair_1) + given
-    chip_sum = chip_sum.reshape(SIDE, width // wide_count, columns)
-    pieces = [send(chip_sum[j].astype(BF16), column_map(STEPS[j])) for j in (1, 2, 3)]
-    total = after(parts[0], pair_1)
+    total = after(parts[0], keep)
     for share in shares:
         total = total + share
     total = total.reshape(SIDE, rows_here, width)
-    tails = [send(total[j], first_line(-STEPS[j])) for j in (1, 2, 3)]
-    grad_2, pairs = fine_second(
-        got_2, fine_weight, label_2, pair_1, order, after(column_ids, total, chip_sum)
-    )
-    pairs = pairs.reshape(owners, -1, 128)
-    back = lax.all_to_all(pairs, AXES, split_axis=0, concat_axis=0, tiled=True)
-
-    new_coarse = BETA * after(coarse_moment, pairs) + chip_sum[0]
+    tails = [send(total[j].astype(BF16), first_line(-STEPS[j])) for j in (1, 2, 3)]
+    chip_sum = after(keep, total) + given
+    chip_sum = chip_sum.reshape(SIDE, width // wide_count, columns)
+    pieces = [send(chip_sum[j].astype(BF16), column_map(STEPS[j])) for j in (1, 2, 3)]
+    new_coarse = BETA * coarse_moment + chip_sum[0]
     for piece in pieces:
         new_coarse = new_coarse + piece.astype(F32)
-    blocks = after(blocks, pairs)
-    every = jnp.arange(owners, dtype=jnp.int32)
-    own_hit = jnp.any(blocks.T[None] == every[:, None, None], axis=1)
-    own_place = jnp.dot(own_hit.astype(BF16), before, preferred_element_type=F32)
-    own_place = own_place.T.astype(jnp.int32)
-    own_slots = blocks * capacity + jnp.sum(
-        jnp.where(blocks[:, :, None] == every[None, None, :], own_place[:, None, :], 0), axis=2
-    )
-
     new_fine = outer(
-        after(column_ids, pairs), [got_1, got_2], [grad_1, grad_2], fine_moment
+        after(column_ids, chip_sum), [got_1, got_2], [grad_1, grad_2], fine_moment
     )
     result = finish(total, tails, own_slots, back.reshape(-1, 128))
     return (result, new_coarse, new_fine)

time: 192 us -> 218 us (1.14)
  the two profiles are of different devices: /device:TPU:32 before, /device:TPU:31 now
where the time goes in v1:
time: 218 us; the launch traced here: 215 us
  Pallas kernels  81.5 us (37%)
  waiting for transfers between devices  64.6 us (30%)
  starting transfers between devices  48.3 us (22%)
  local copies, waits for them, and re-layouts  11 us (5%)
  other arithmetic  8.24 us (4%)
    ppermute x22, waiting for transfers between devices, send(): return lax.ppermute(value, AXES, pairs)  59.9 us
    ppermute x22, starting transfers between devices, send(): return lax.ppermute(value, AXES, pairs)  26.2 us
    pallas_call x4, Pallas kernels, coarse(): call(functools.partial(coarse_body, steps, top), (steps,), [whole(rows),...  15.1 us
    pallas_call x1, Pallas kernels, fine_second(): call(functools.partial(fine_second_body, steps), (steps,), [whole(rows),...  13.8 us
    pallas_call x1, Pallas kernels, outer(): call(functools.partial(outer_body, len(lefts), moment is not None), (widt...  13.7 us
    all_to_all x2, starting transfers between devices, swap_wide(): lax.all_to_all(value, 'wide', split_axis=0, concat_axis=0, tiled=True)  13.4 us
    pallas_call x1, Pallas kernels, ordered_outer(): pl.pallas_call(functools.partial(ordered_outer_body, len(lefts), half), n...  11.6 us
    pallas_call x1, Pallas kernels, fine_first(): call(functools.partial(fine_first_body, steps, wide_count, group), (steps...  11.2 us
  transfers between devices with their start and end apart: 25, of which 9 were waited for; matrix products, arithmetic and copies ran while one was open for 4% of the time, Pallas kernels for 24%

profile of v1, /device:TPU:31, one launch (start us, length us, event | category | flops | bytes accessed | tf_op | source)
XLA Modules:
  0.0 214.6 jit_solution(3421364415304623721)
XLA Ops:
  6.2 4.2 %collective-permute-done.1 = bf16[128,1024]{1,0:T(8,128)(2,1)S(1)} collective-permute-done((bf16[128,1024]{1,0:T(8,128)(2,1)}, bf16[128,1024]{1,0:T(8,128)(2,1)S(1)}, u32[]{:S(2)}, u32[]{:S(2)}) %collective-permute-start.1) | collective-permute-done | bytes 262176 | tf_op jit(solution)/shard_map/ppermute | solution.py:48
  10.5 4.1 %collective-permute-start.10 = (bf16[512,1024]{1,0:T(8,128)(2,1)S(1)}, bf16[512,1024]{1,0:T(8,128)(2,1)S(1)}, u32[]{:S(2)}, u32[]{:S(2)}) collective-permute-start(bf16[512,1024]{1,0:T(8,128)(2,1)S(1)} %constant_dynamic-update-slice_fusion.row_ref.refs_0_.refs_1_), channel_id=1, source_target_pairs={{0,12},{1,13},{2,14},{3,15},{4,0},{5,1},{6,2},{7,3},{8,4},{9,5},{1... | collective-permute-start | bytes 3145736 | tf_op jit(solution)/shard_map/ppermute | solution.py:48
  14.8 2.7 %collective-permute-start.3 = (s32[24,128]{1,0:T(8,128)S(1)}, s32[24,128]{1,0:T(8,128)S(1)}, u32[]{:S(2)}, u32[]{:S(2)}) collective-permute-start(s32[24,128]{1,0:T(8,128)S(1)} %get-tuple-element.88), channel_id=1, source_target_pairs={{0,1},{1,2},{2,3},{3,0},{4,5},{5,6},{6,7},{7,4},{8,9},{9,10},{10,1... | collective-permute-start | bytes 36872 | tf_op jit(solution)/shard_map/ppermute | solution.py:48
  18.8 2.8 %collective-permute-done.5 = s32[24,128]{1,0:T(8,128)S(1)} collective-permute-done((s32[24,128]{1,0:T(8,128)S(1)}, s32[24,128]{1,0:T(8,128)S(1)}, u32[]{:S(2)}, u32[]{:S(2)}) %collective-permute-start.5) | collective-permute-done | bytes 12320 | tf_op jit(solution)/shard_map/ppermute | solution.py:48
  26.4 4.0 %shard_map.121 = (bf16[512,1024]{1,0:T(8,128)(2,1)}, f32[512,1024]{1,0:T(8,128)}) custom-call(bf16[512,1024]{1,0:T(8,128)(2,1)S(1)} %constant_dynamic-update-slice_fusion.row_ref.refs_0_.refs_1_, bf16[1024,1024]{1,0:T(8,128)(2,1)S(1)} %copy-done.13, s32[4,24,128]{2,1,0:T(8,128)S(1)} %pad_add_fusion.note_ref.refs_0_, ...), custom_call_target="tpu_custom_call" | custom-call | flops 2147483648 | bytes 2147483 | tf_op jit(solution)/shard_map/pallas_call | solution.py:258
  34.5 2.6 %shard_map.124.refs_0_ = bf16[8,88,1024]{2,1,0:T(8,128)(2,1)} custom-call(bf16[512,1024]{1,0:T(8,128)(2,1)} %copy-done.1, s32[8,512]{1,0:T(8,128)S(1)} %copy-done.11, bf16[8,88,1024]{2,1,0:T(8,128)(2,1)} %shard_map.123.refs_0_), custom_call_target="tpu_custom_call", output_to_operand_aliasing={{}: (2, {})} | custom-call | flops 335544320 | bytes 335544 | tf_op jit(solution)/shard_map/pallas_call | solution.py:116
  38.5 2.6 %shard_map.125 = bf16[8,88,1024]{2,1,0:T(8,128)(2,1)} custom-call(bf16[512,1024]{1,0:T(8,128)(2,1)} %copy-done.5, s32[8,512]{1,0:T(8,128)S(1)} %copy-done.10, bf16[8,88,1024]{2,1,0:T(8,128)(2,1)} %shard_map.124.refs_0_), custom_call_target="tpu_custom_call", output_to_operand_aliasing={{}: (2, {})} | custom-call | flops 335544320 | bytes 335544 | tf_op jit(solution)/shard_map/pallas_call | solution.py:116
  41.2 8.5 %all-to-all-start.1 = ((bf16[8,88,1024]{2,1,0:T(8,128)(2,1)}), bf16[8,88,1024]{2,1,0:T(8,128)(2,1)}, u32[]{:S(2)}, u32[]{:S(2)}) async-start(bf16[8,88,1024]{2,1,0:T(8,128)(2,1)} %shard_map.125), calls=%async_computation.1 | async-start | bytes 2883584 | tf_op jit(solution)/shard_map/all_to_all | solution.py:56
  51.2 3.7 %shard_map.126 = (bf16[512,1024]{1,0:T(8,128)(2,1)}, bf16[512,1024]{1,0:T(8,128)(2,1)}) custom-call(bf16[512,1024]{1,0:T(8,128)(2,1)S(1)} %copy-done.6, bf16[1024,1024]{1,0:T(8,128)(2,1)S(1)} %copy-done.14, s32[4,24,128]{2,1,0:T(8,128)S(1)} %collective-permute-done.6.refs_1_.note_ref, f32[1,1024]{1,0:T(1,128)S(1)} %add_convert_fusion.id_ref.token_ref), custom_call_target="tpu_custom_call" | custom-call | flops 2147483648 | bytes 2147483 | tf_op jit(solution)/shard_map/pallas_call | solution.py:258
  54.9 3.7 %shard_map.127 = (bf16[512,1024]{1,0:T(8,128)(2,1)}, bf16[512,1024]{1,0:T(8,128)(2,1)}) custom-call(bf16[512,1024]{1,0:T(8,128)(2,1)S(1)} %collective-permute-done.10.row_ref.refs_4_.refs_5_, bf16[1024,1024]{1,0:T(8,128)(2,1)S(1)} %copy-done.14, s32[4,24,128]{2,1,0:T(8,128)S(1)} %collective-permute-done.7.refs_2_.note_ref, ...), custom_call_target="tpu_custom_call" | custom-call | flops 2147483648 | bytes 2147483 | tf_op jit(solution)/shard_map/pallas_call | solution.py:258
  66.2 3.7 %shard_map.130 = (bf16[512,1024]{1,0:T(8,128)(2,1)}, bf16[512,1024]{1,0:T(8,128)(2,1)}) custom-call(bf16[512,1024]{1,0:T(8,128)(2,1)S(1)} %copy-done.3, bf16[1024,1024]{1,0:T(8,128)(2,1)S(1)} %copy-done.15, s32[4,24,128]{2,1,0:T(8,128)S(1)} %collective-permute-done.8.refs_3_.note_ref, f32[1,1024]{1,0:T(1,128)S(1)} %add_convert_fusion.id_ref.token_ref), custom_call_target="tpu_custom_call" | custom-call | flops 2147483648 | bytes 2147483 | tf_op jit(solution)/shard_map/pallas_call | solution.py:258
  69.9 5.0 %all-to-all-start = ((bf16[8,80,1024]{2,1,0:T(8,128)(2,1)}), bf16[8,80,1024]{2,1,0:T(8,128)(2,1)S(1)}, u32[]{:S(2)}, u32[]{:S(2)}) async-start(bf16[8,80,1024]{2,1,0:T(8,128)(2,1)} %shard_map.129), calls=%async_computation | async-start | bytes 2621440 | tf_op jit(solution)/shard_map/all_to_all | solution.py:56
  75.1 11.2 %shard_map.131 = (bf16[704,2048]{1,0:T(8,128)(2,1)}, bf16[704,1024]{1,0:T(8,128)(2,1)}, f32[640,1]{1,0:T(8,128)}) custom-call(bf16[704,1024]{1,0:T(8,128)(2,1)} %bitcast.8.row_ref.refs_0_, bf16[1,1024,2048]{2,1,0:T(8,128)(2,1)} %weight_ref.11, s32[1,128]{1,0:T(1,128)S(1)} %broadcast_in_dim.41.seat_ref), custom_call_target="tpu_custom_call" | custom-call | flops 5905580032 | bytes 5905580 | tf_op jit(solution)/shard_map/pallas_call | solution.py:339
  86.3 4.7 %all-to-all-done = bf16[8,80,1024]{2,1,0:T(8,128)(2,1)S(1)} async-done(((bf16[8,80,1024]{2,1,0:T(8,128)(2,1)}), bf16[8,80,1024]{2,1,0:T(8,128)(2,1)S(1)}, u32[]{:S(2)}, u32[]{:S(2)}) %all-to-all-start) | async-done | bytes 1310752 | tf_op jit(solution)/shard_map/all_to_all | solution.py:56
  92.0 13.8 %shard_map.132 = (bf16[640,2048]{1,0:T(8,128)(2,1)}, bf16[10240,128]{1,0:T(8,128)(2,1)}) custom-call(bf16[640,1024]{1,0:T(8,128)(2,1)} %bitcast.15, bf16[1,1024,2048]{2,1,0:T(8,128)(2,1)} %weight_ref.11, f32[640,1]{1,0:T(8,128)} %get-tuple-element.56.label_ref, bf16[704,1024]{1,0:T(8,128)(2,1)} %get-tuple-element.57.pair_ref, s32[8,160]{1,0:T(8,128)S(1)} %stack.31.order_ref, ...), custom_call_target="tpu_custom_call" | custom-call | flops 5368709120 | bytes 5368709 | tf_op jit(solution)/shard_map/pallas_call | solution.py:396
  105.9 11.6 %ordered_outer.1 = (f32[512,1024]{1,0:T(8,128)}, f32[512,1024]{1,0:T(8,128)}) custom-call(s32[8]{0:T(128)S(1)} %pad_add_fusion.1.order_ref, f32[1,1024]{1,0:T(1,128)S(1)} %add_convert_fusion.id_ref.token_ref, bf16[512,1024]{1,0:T(8,128)(2,1)} %copy-done.1, bf16[512,1024]{1,0:T(8,128)(2,1)} %copy-done.1, bf16[512,1024]{1,0:T(8,128)(2,1)} %copy-done.5, ...), custom_call_target="tpu_custom_call" | custom-call | flops 4294967296 | bytes 16777216 | tf_op jit(solution)/shard_map/ordered_outer/pallas_call | solution.py:546
  118.5 2.8 %collective-permute-start.12 = (bf16[512,1024]{1,0:T(8,128)(2,1)}, bf16[512,1024]{1,0:T(8,128)(2,1)}, u32[]{:S(2)}, u32[]{:S(2)}) collective-permute-start(bf16[512,1024]{1,0:T(8,128)(2,1)} %get-tuple-element.67), channel_id=1, source_target_pairs={{0,12},{1,13},{2,14},{3,15},{4,0},{5,1},{6,2},{7,3},{8,4},{9,5},{1... | collective-permute-start | bytes 3145736 | tf_op jit(solution)/shard_map/ppermute | solution.py:48
  122.5 8.6 %all-to-all-start.2 = ((bf16[128,80,128]{2,1,0:T(8,128)(2,1)}), bf16[128,80,128]{2,1,0:T(8,128)(2,1)S(1)}, u32[]{:S(2)}, u32[]{:S(2)}) async-start(bf16[128,80,128]{2,1,0:T(8,128)(2,1)} %bitcast.17), calls=%async_computation.2 | async-start | bytes 5242880 | tf_op jit(solution)/shard_map/all_to_all | solution.py:651
  131.1 43.5 %collective-permute-done.12 = bf16[512,1024]{1,0:T(8,128)(2,1)} collective-permute-done((bf16[512,1024]{1,0:T(8,128)(2,1)}, bf16[512,1024]{1,0:T(8,128)(2,1)}, u32[]{:S(2)}, u32[]{:S(2)}) %collective-permute-start.12) | collective-permute-done | bytes 1048608 | tf_op jit(solution)/shard_map/ppermute | solution.py:48
  176.6 4.7 %fusion.14 = (bf16[512,1024]{1,0:T(8,128)(2,1)S(1)}, f32[512,1024]{1,0:T(8,128)}) fusion(bf16[512,1024]{1,0:T(8,128)(2,1)} %collective-permute-done.14, bf16[512,1024]{1,0:T(8,128)(2,1)} %collective-permute-done.13, f32[512,1024]{1,0:T(8,128)} %get-tuple-element.66, bf16[512,1024]{1,0:T(8,128)(2,1)} %collective-permute-done.12), kind=kLoop, calls=%fused_computation.54 | loop fusion | flops 3670016 | bytes 8388608 | tf_op jit(solution)/shard_map/convert.5
  181.4 3.5 %collective-permute-start.17 = (bf16[128,1024]{1,0:T(8,128)(2,1)S(1)}, bf16[128,1024]{1,0:T(8,128)(2,1)S(1)}, u32[]{:S(2)}, u32[]{:S(2)}) collective-permute-start(bf16[128,1024]{1,0:T(8,128)(2,1)S(1)} %get-tuple-element.84), channel_id=1, source_target_pairs={{0,2},{1,3},{2,0},{3,1},{4,6},{5,7},{6,4},{7,5},{8,10},{9,11},{10,... | collective-permute-start | bytes 786440 | tf_op jit(solution)/shard_map/ppermute | solution.py:48
  189.2 13.7 %shard_map.134 = f32[1,1024,2048]{2,1,0:T(8,128)} custom-call(f32[1,1024]{1,0:T(1,128)S(1)} %add_convert_fusion.id_ref.token_ref, bf16[704,1024]{1,0:T(8,128)(2,1)} %bitcast.8.row_ref.refs_0_, bf16[640,1024]{1,0:T(8,128)(2,1)} %bitcast.16, bf16[704,2048]{1,0:T(8,128)(2,1)} %get-tuple-element.73.refs_2_, bf16[640,2048]{1,0:T(8,128)(2,1)} %get-tuple-element.74.refs_3_, ...), custom_call_target="tpu_custom_call" | custom-call | flops 5637144576 | bytes 5637144 | tf_op jit(solution)/shard_map/pallas_call | solution.py:491
  205.3 4.1 %collective-permute-done.15.one_ref = bf16[128,1024]{1,0:T(8,128)(2,1)S(1)} collective-permute-done((bf16[128,1024]{1,0:T(8,128)(2,1)S(1)}, bf16[128,1024]{1,0:T(8,128)(2,1)S(1)}, u32[]{:S(2)}, u32[]{:S(2)}) %collective-permute-start.15) | collective-permute-done | bytes 262176 | tf_op jit(solution)/shard_map/ppermute | solution.py:48
  210.9 3.6 %shard_map.133 = f32[128,1024]{1,0:T(8,128)} custom-call(f32[4,128,1024]{2,1,0:T(8,128)S(1)} %bitcast.14, bf16[128,1024]{1,0:T(8,128)(2,1)S(1)} %collective-permute-done.15.one_ref, bf16[128,1024]{1,0:T(8,128)(2,1)S(1)} %collective-permute-done.16.two_ref, bf16[128,1024]{1,0:T(8,128)(2,1)S(1)} %collective-permute-done.17.three_ref, f32[8,128]{1,0:T(8,128)S(1)} %copy-done.12, ...), custom_call_target="tpu_custom_call" | custom-call | flops 335544320 | bytes 335544 | tf_op jit(solution)/shard_map/pallas_call | solution.py:442
  (109 shorter events, 40.2 us)
Async XLA Ops:
  0.7 5.5 %collective-permute-start = (bf16[128,1024]{1,0:T(8,128)(2,1)}, bf16[128,1024]{1,0:T(8,128)(2,1)S(1)}, u32[]{:S(2)}, u32[]{:S(2)}) collective-permute-start(bf16[128,1024]{1,0:T(8,128)(2,1)} %param.10), channel_id=1, source_target_pairs={{0,1},{1,2},{2,3},{3,0},{4,5},{5,6},{6,7},{7,4},{8,9},{9,10},{10,1... | collective-permute-start | bytes 786440 | tf_op jit(solution)/shard_map/ppermute | solution.py:48
  0.9 9.5 %collective-permute-start.1 = (bf16[128,1024]{1,0:T(8,128)(2,1)}, bf16[128,1024]{1,0:T(8,128)(2,1)S(1)}, u32[]{:S(2)}, u32[]{:S(2)}) collective-permute-start(bf16[128,1024]{1,0:T(8,128)(2,1)} %param.10), channel_id=1, source_target_pairs={{0,3},{1,0},{2,1},{3,2},{4,7},{5,4},{6,5},{7,6},{8,11},{9,8},{10,9... | collective-permute-start | bytes 786440 | tf_op jit(solution)/shard_map/ppermute | solution.py:48
  2.2 8.2 %collective-permute-start.2 = (bf16[128,1024]{1,0:T(8,128)(2,1)}, bf16[128,1024]{1,0:T(8,128)(2,1)S(1)}, u32[]{:S(2)}, u32[]{:S(2)}) collective-permute-start(bf16[128,1024]{1,0:T(8,128)(2,1)} %param.10), channel_id=1, source_target_pairs={{0,2},{1,3},{2,0},{3,1},{4,6},{5,7},{6,4},{7,5},{8,10},{9,11},{10,... | collective-permute-start | bytes 786440 | tf_op jit(solution)/shard_map/ppermute | solution.py:48
  10.5 26.7 %collective-permute-start.10 = (bf16[512,1024]{1,0:T(8,128)(2,1)S(1)}, bf16[512,1024]{1,0:T(8,128)(2,1)S(1)}, u32[]{:S(2)}, u32[]{:S(2)}) collective-permute-start(bf16[512,1024]{1,0:T(8,128)(2,1)S(1)} %constant_dynamic-update-slice_fusion.row_ref.refs_0_.refs_1_), channel_id=1, source_target_pairs={{0,12},{1,13},{2,14},{3,15},{4,0},{5,1},{6,2},{7,3},{8,4},{9,5},{1... | collective-permute-start | bytes 3145736 | tf_op jit(solution)/shard_map/ppermute | solution.py:48
  14.6 22.6 %collective-permute-start.9 = (bf16[512,1024]{1,0:T(8,128)(2,1)S(1)}, bf16[512,1024]{1,0:T(8,128)(2,1)S(1)}, u32[]{:S(2)}, u32[]{:S(2)}) collective-permute-start(bf16[512,1024]{1,0:T(8,128)(2,1)S(1)} %constant_dynamic-update-slice_fusion.row_ref.refs_0_.refs_1_), channel_id=1, source_target_pairs={{0,4},{1,5},{2,6},{3,7},{4,8},{5,9},{6,10},{7,11},{8,12},{9,13},{1... | collective-permute-start | bytes 3145736 | tf_op jit(solution)/shard_map/ppermute | solution.py:48
  14.7 4.1 %collective-permute-start.4 = (s32[24,128]{1,0:T(8,128)S(1)}, s32[24,128]{1,0:T(8,128)S(1)}, u32[]{:S(2)}, u32[]{:S(2)}) collective-permute-start(s32[24,128]{1,0:T(8,128)S(1)} %get-tuple-element.88), channel_id=1, source_target_pairs={{0,3},{1,0},{2,1},{3,2},{4,7},{5,4},{6,5},{7,6},{8,11},{9,8},{10,9... | collective-permute-start | bytes 36872 | tf_op jit(solution)/shard_map/ppermute | solution.py:48
  17.4 4.2 %collective-permute-start.5 = (s32[24,128]{1,0:T(8,128)S(1)}, s32[24,128]{1,0:T(8,128)S(1)}, u32[]{:S(2)}, u32[]{:S(2)}) collective-permute-start(s32[24,128]{1,0:T(8,128)S(1)} %get-tuple-element.88), channel_id=1, source_target_pairs={{0,2},{1,3},{2,0},{3,1},{4,6},{5,7},{6,4},{7,5},{8,10},{9,11},{10,... | collective-permute-start | bytes 36872 | tf_op jit(solution)/shard_map/ppermute | solution.py:48
  21.6 9.0 %collective-permute-start.8 = (s32[4,24,128]{2,1,0:T(8,128)S(1)}, s32[4,24,128]{2,1,0:T(8,128)S(1)}, u32[]{:S(2)}, u32[]{:S(2)}) collective-permute-start(s32[4,24,128]{2,1,0:T(8,128)S(1)} %pad_add_fusion.note_ref.refs_0_), channel_id=1, source_target_pairs={{0,8},{1,9},{2,10},{3,11},{4,12},{5,13},{6,14},{7,15},{8,0},{9,1},... | collective-permute-start | bytes 147464 | tf_op jit(solution)/shard_map/ppermute | solution.py:48
  22.9 7.7 %collective-permute-start.7 = (s32[4,24,128]{2,1,0:T(8,128)S(1)}, s32[4,24,128]{2,1,0:T(8,128)S(1)}, u32[]{:S(2)}, u32[]{:S(2)}) collective-permute-start(s32[4,24,128]{2,1,0:T(8,128)S(1)} %pad_add_fusion.note_ref.refs_0_), channel_id=1, source_target_pairs={{0,12},{1,13},{2,14},{3,15},{4,0},{5,1},{6,2},{7,3},{8,4},{9,5},{1... | collective-permute-start | bytes 147464 | tf_op jit(solution)/shard_map/ppermute | solution.py:48
  24.4 6.7 %collective-permute-start.6 = (s32[4,24,128]{2,1,0:T(8,128)S(1)}, s32[4,24,128]{2,1,0:T(8,128)S(1)}, u32[]{:S(2)}, u32[]{:S(2)}) collective-permute-start(s32[4,24,128]{2,1,0:T(8,128)S(1)} %pad_add_fusion.note_ref.refs_0_), channel_id=1, source_target_pairs={{0,4},{1,5},{2,6},{3,7},{4,8},{5,9},{6,10},{7,11},{8,12},{9,13},{1... | collective-permute-start | bytes 147464 | tf_op jit(solution)/shard_map/ppermute | solution.py:48
  37.1 24.2 %collective-permute-start.11 = (bf16[512,1024]{1,0:T(8,128)(2,1)}, bf16[512,1024]{1,0:T(8,128)(2,1)S(1)}, u32[]{:S(2)}, u32[]{:S(2)}) collective-permute-start(bf16[512,1024]{1,0:T(8,128)(2,1)} %copy-done.1), channel_id=1, source_target_pairs={{0,8},{1,9},{2,10},{3,11},{4,12},{5,13},{6,14},{7,15},{8,0},{9,1},... | collective-permute-start | bytes 3145736 | tf_op jit(solution)/shard_map/ppermute | solution.py:48
  41.2 28.7 %all-to-all-start.1 = ((bf16[8,88,1024]{2,1,0:T(8,128)(2,1)}), bf16[8,88,1024]{2,1,0:T(8,128)(2,1)}, u32[]{:S(2)}, u32[]{:S(2)}) async-start(bf16[8,88,1024]{2,1,0:T(8,128)(2,1)} %shard_map.125), calls=%async_computation.1 | async-start | bytes 2883584 | tf_op jit(solution)/shard_map/all_to_all | solution.py:56
  69.9 21.1 %all-to-all-start = ((bf16[8,80,1024]{2,1,0:T(8,128)(2,1)}), bf16[8,80,1024]{2,1,0:T(8,128)(2,1)S(1)}, u32[]{:S(2)}, u32[]{:S(2)}) async-start(bf16[8,80,1024]{2,1,0:T(8,128)(2,1)} %shard_map.129), calls=%async_computation | async-start | bytes 2621440 | tf_op jit(solution)/shard_map/all_to_all | solution.py:56
  117.5 67.5 %collective-permute-start.18 = (f32[512,1024]{1,0:T(8,128)}, f32[512,1024]{1,0:T(8,128)}, u32[]{:S(2)}, u32[]{:S(2)}) collective-permute-start(f32[512,1024]{1,0:T(8,128)} %get-tuple-element.72), channel_id=1, source_target_pairs={{0,16},{1,17},{2,18},{3,19},{4,20},{5,21},{6,22},{7,23},{8,24},{9,... | collective-permute-start | bytes 6291464 | tf_op jit(solution)/shard_map/ppermute | solution.py:48
  118.5 56.1 %collective-permute-start.12 = (bf16[512,1024]{1,0:T(8,128)(2,1)}, bf16[512,1024]{1,0:T(8,128)(2,1)}, u32[]{:S(2)}, u32[]{:S(2)}) collective-permute-start(bf16[512,1024]{1,0:T(8,128)(2,1)} %get-tuple-element.67), channel_id=1, source_target_pairs={{0,12},{1,13},{2,14},{3,15},{4,0},{5,1},{6,2},{7,3},{8,4},{9,5},{1... | collective-permute-start | bytes 3145736 | tf_op jit(solution)/shard_map/ppermute | solution.py:48
  121.3 53.4 %collective-permute-start.13 = (bf16[512,1024]{1,0:T(8,128)(2,1)}, bf16[512,1024]{1,0:T(8,128)(2,1)}, u32[]{:S(2)}, u32[]{:S(2)}) collective-permute-start(bf16[512,1024]{1,0:T(8,128)(2,1)} %get-tuple-element.68), channel_id=1, source_target_pairs={{0,4},{1,5},{2,6},{3,7},{4,8},{5,9},{6,10},{7,11},{8,12},{9,13},{1... | collective-permute-start | bytes 3145736 | tf_op jit(solution)/shard_map/ppermute | solution.py:48
  121.3 55.3 %collective-permute-start.14 = (bf16[512,1024]{1,0:T(8,128)(2,1)}, bf16[512,1024]{1,0:T(8,128)(2,1)}, u32[]{:S(2)}, u32[]{:S(2)}) collective-permute-start(bf16[512,1024]{1,0:T(8,128)(2,1)} %get-tuple-element.69), channel_id=1, source_target_pairs={{0,8},{1,9},{2,10},{3,11},{4,12},{5,13},{6,14},{7,15},{8,0},{9,1},... | collective-permute-start | bytes 3145736 | tf_op jit(solution)/shard_map/ppermute | solution.py:48
  122.5 86.9 %all-to-all-start.2 = ((bf16[128,80,128]{2,1,0:T(8,128)(2,1)}), bf16[128,80,128]{2,1,0:T(8,128)(2,1)S(1)}, u32[]{:S(2)}, u32[]{:S(2)}) async-start(bf16[128,80,128]{2,1,0:T(8,128)(2,1)} %bitcast.17), calls=%async_computation.2 | async-start | bytes 5242880 | tf_op jit(solution)/shard_map/all_to_all | solution.py:651
  181.4 23.9 %collective-permute-start.17 = (bf16[128,1024]{1,0:T(8,128)(2,1)S(1)}, bf16[128,1024]{1,0:T(8,128)(2,1)S(1)}, u32[]{:S(2)}, u32[]{:S(2)}) collective-permute-start(bf16[128,1024]{1,0:T(8,128)(2,1)S(1)} %get-tuple-element.84), channel_id=1, source_target_pairs={{0,2},{1,3},{2,0},{3,1},{4,6},{5,7},{6,4},{7,5},{8,10},{9,11},{10,... | collective-permute-start | bytes 786440 | tf_op jit(solution)/shard_map/ppermute | solution.py:48
  184.9 20.3 %collective-permute-start.16 = (bf16[128,1024]{1,0:T(8,128)(2,1)S(1)}, bf16[128,1024]{1,0:T(8,128)(2,1)S(1)}, u32[]{:S(2)}, u32[]{:S(2)}) collective-permute-start(bf16[128,1024]{1,0:T(8,128)(2,1)S(1)} %get-tuple-element.85), channel_id=1, source_target_pairs={{0,1},{1,2},{2,3},{3,0},{4,5},{5,6},{6,7},{7,4},{8,9},{9,10},{10,1... | collective-permute-start | bytes 786440 | tf_op jit(solution)/shard_map/ppermute | solution.py:48
  187.3 15.5 %collective-permute-start.19 = (bf16[128,1024]{1,0:T(8,128)(2,1)S(1)}, bf16[128,1024]{1,0:T(8,128)(2,1)S(1)}, u32[]{:S(2)}, u32[]{:S(2)}) collective-permute-start(bf16[128,1024]{1,0:T(8,128)(2,1)S(1)} %get-tuple-element.81), channel_id=1, source_target_pairs={{0,32},{1,33},{2,34},{3,35},{4,36},{5,37},{6,38},{7,39},{8,40},{9,... | collective-permute-start | bytes 786440 | tf_op jit(solution)/shard_map/ppermute | solution.py:48
  188.4 15.9 %collective-permute-start.21 = (bf16[128,1024]{1,0:T(8,128)(2,1)S(1)}, bf16[128,1024]{1,0:T(8,128)(2,1)S(1)}, u32[]{:S(2)}, u32[]{:S(2)}) collective-permute-start(bf16[128,1024]{1,0:T(8,128)(2,1)S(1)} %get-tuple-element.82), channel_id=1, source_target_pairs={{0,64},{1,65},{2,66},{3,67},{4,68},{5,69},{6,70},{7,71},{8,72},{9,... | collective-permute-start | bytes 786440 | tf_op jit(solution)/shard_map/ppermute | solution.py:48
  188.9 15.3 %collective-permute-start.20 = (bf16[128,1024]{1,0:T(8,128)(2,1)S(1)}, bf16[128,1024]{1,0:T(8,128)(2,1)S(1)}, u32[]{:S(2)}, u32[]{:S(2)}) collective-permute-start(bf16[128,1024]{1,0:T(8,128)(2,1)S(1)} %get-tuple-element.83), channel_id=1, source_target_pairs={{0,96},{1,97},{2,98},{3,99},{4,100},{5,101},{6,102},{7,103},{8,104... | collective-permute-start | bytes 786440 | tf_op jit(solution)/shard_map/ppermute | solution.py:48
  202.8 6.5 %collective-permute-start.15 = (bf16[128,1024]{1,0:T(8,128)(2,1)S(1)}, bf16[128,1024]{1,0:T(8,128)(2,1)S(1)}, u32[]{:S(2)}, u32[]{:S(2)}) collective-permute-start(bf16[128,1024]{1,0:T(8,128)(2,1)S(1)} %get-tuple-element.86), channel_id=1, source_target_pairs={{0,3},{1,0},{2,1},{3,2},{4,7},{5,4},{6,5},{7,6},{8,11},{9,8},{10,9... | collective-permute-start | bytes 786440 | tf_op jit(solution)/shard_map/ppermute | solution.py:48
  (24 other events, 157.8 us)
